TPU v7x, 512 devices: a whole 4x4x16 slice. The times are simulated.
512 devices in a mesh: dp: 32 (over x_hi, z), spatial: 16 (over x_lo, y, core).
Axes of the slice: x: 4 (x_hi: 2, x_lo: 2; x = x_hi * 2 + x_lo), y: 4, z: 16, core: 2. Of those that a mesh axis runs over, the one named last changes fastest.
Arguments:
- latents: bfloat16 [64, 32, 32, 640], P('dp', 'spatial'), may hold values from -16 to 16
- plan: bfloat16 [64, 256, 640], P('dp', 'spatial'), may hold values from -45 to 45
- conv_weight: bfloat16 [9, 640, 640], P(None, 'dp'), may hold values from -0.078125 to 0.078125
- gn_gain: float32 [640], replicated, may hold values from 0.5 to 2
- attn_weights: bfloat16 [4, 640, 640], P(None, 'dp'), may hold values from -0.25 to 0.25
- cotangent: bfloat16 [64, 32, 32, 640], P('dp', 'spatial'), may hold values from -6 to 6
Outputs:
- block_out: bfloat16 [64, 32, 32, 640], P('dp', 'spatial')
- weight_grads: float32 [640, 2, 640], P('dp')
All inputs are finite; a program needn't handle non-finite values.
Results may differ from a plain program's by a relative error of at most 0.03.
The roundings to bfloat16 on the way count: a program that leaves them out, or rounds other values in their place, can miss the bound.
Values may be sent and summed in bfloat16 or wider, within the bound.
A program may use at most 64 MiB of HBM per device.

v0:
```python
import math

import jax
import jax.numpy as jnp
from jax import lax
from jax.sharding import PartitionSpec as P

GROUPS = 32
HEAD = 64


eps_norm = 1e-05


def with_halo(cells, sides, width):
    for axis, dim in sides:
        count = lax.axis_size(axis)
        ends = count - 1
        head = lax.slice_in_dim(cells, 0, width, axis=dim)
        tail = lax.slice_in_dim(cells, cells.shape[dim] - width, cells.shape[dim], axis=dim)
        cells = jnp.concatenate(
            [
                lax.ppermute(tail, axis, [(i, (i + 1) % count) for i in range(ends)]),
                cells,
                lax.ppermute(head, axis, [((i + 1) % count, i) for i in range(ends)]),
            ],
            axis=dim,
        )
    return cells


def body(latents, plan, conv_weight, gn_gain, attn_weights, cotangent):
    images, band_rows, columns, channels = latents.shape
    heads = channels // HEAD
    per_group = channels // GROUPS
    tokens_here = images * band_rows * columns
    scale = 1.0 / math.sqrt(HEAD)
    flat_input = latents.astype(jnp.float32).reshape(images, band_rows * columns, GROUPS, per_group)
    first_sums = jnp.sum(flat_input, axis=(1, 3))
    second_sums = jnp.sum(flat_input * flat_input, axis=(1, 3))
    first_sums, second_sums = lax.psum((first_sums, second_sums), "spatial")
    counted = float(band_rows * lax.axis_size("spatial") * columns * per_group)
    means = first_sums / counted
    variance = second_sums / counted - means * means
    inverse = lax.rsqrt(variance + eps_norm)
    normed = (flat_input - means[:, None, :, None]) * inverse[:, None, :, None]
    normed = normed.reshape(images, band_rows, columns, channels) * gn_gain
    hidden = jax.nn.silu(normed).astype(jnp.bfloat16)
    padded = with_halo(hidden, (("spatial", 1),), 1)
    padded = jnp.pad(padded, ((0, 0), (0, 0), (1, 1), (0, 0)))
    tapped = jnp.stack(
        [
            padded[:, offset_y : offset_y + band_rows, offset_x : offset_x + columns].reshape(
                tokens_here, channels
            )
            for offset_y in range(3)
            for offset_x in range(3)
        ],
        1,
    )
    conv_sum = jnp.einsum(
        "ntc,tcd->nd",
        tapped,
        lax.all_gather(conv_weight, "dp", axis=1, tiled=True),
        preferred_element_type=jnp.float32,
    )
    mixed = (latents.reshape(tokens_here, channels).astype(jnp.float32) + conv_sum).astype(
        jnp.bfloat16
    )
    weights = lax.all_gather(attn_weights, "dp", axis=1, tiled=True)
    weight_q = weights[0]
    weight_k = weights[1]
    weight_v = weights[2]
    weight_o = weights[3]
    queries = jnp.dot(mixed, weight_q, preferred_element_type=jnp.float32).astype(jnp.bfloat16)
    plan_all = lax.all_gather(plan, "spatial", axis=1, tiled=True)
    plan_flat = plan_all.reshape(-1, channels)
    keys_all = jnp.dot(plan_flat, weight_k, preferred_element_type=jnp.float32).astype(jnp.bfloat16)
    values_all = jnp.dot(plan_flat, weight_v, preferred_element_type=jnp.float32).astype(
        jnp.bfloat16
    )
    keys_all = keys_all.reshape(images, -1, channels)
    values_all = values_all.reshape(images, -1, channels)
    plan_tokens = keys_all.shape[1]
    query_heads = queries.reshape(images, band_rows * columns, heads, HEAD)
    key_heads = keys_all.reshape(images, plan_tokens, heads, HEAD)
    value_heads = values_all.reshape(images, plan_tokens, heads, HEAD)
    scores = (
        jnp.einsum("bnhe,bmhe->bhnm", query_heads, key_heads, preferred_element_type=jnp.float32)
        * scale
    )
    maxima = jnp.max(scores, axis=-1, keepdims=True)
    expo = jnp.exp(scores - maxima)
    probs = expo / jnp.sum(expo, axis=-1, keepdims=True)
    probs_b = probs.astype(jnp.bfloat16)
    attended = jnp.einsum(
        "bhnm,bmhe->bnhe", probs_b, value_heads, preferred_element_type=jnp.float32
    )
    attended = attended.reshape(tokens_here, channels).astype(jnp.bfloat16)
    result = mixed.astype(jnp.float32) + jnp.dot(
        attended, weight_o, preferred_element_type=jnp.float32
    )
    block_out = result.astype(jnp.bfloat16).reshape(images, band_rows, columns, channels)
    grad_flat = cotangent.reshape(tokens_here, channels)
    grad_att = lax.dot_general(
        grad_flat, weight_o, (((1,), (1,)), ((), ())), preferred_element_type=jnp.float32
    )
    grad_att = grad_att.astype(jnp.bfloat16).reshape(images, band_rows * columns, heads, HEAD)
    dprob = jnp.einsum("bnhe,bmhe->bhnm", grad_att, value_heads, preferred_element_type=jnp.float32)
    dscore = (probs * (dprob - jnp.sum(probs * dprob, axis=-1, keepdims=True)) * scale).astype(
        jnp.bfloat16
    )
    dquery = jnp.einsum("bhnm,bmhe->bnhe", dscore, key_heads, preferred_element_type=jnp.float32)
    dquery = dquery.reshape(tokens_here, channels).astype(jnp.bfloat16)
    total_tokens = images * lax.axis_size("dp") * band_rows * lax.axis_size("spatial") * columns
    factor = 1.0 / math.sqrt(total_tokens)
    contract = (((0,), (0,)), ((), ()))
    grad_query = lax.dot_general(mixed, dquery, contract, preferred_element_type=jnp.float32)
    grad_output = lax.dot_general(attended, grad_flat, contract, preferred_element_type=jnp.float32)
    own_rows = lax.psum_scatter(
        jnp.stack([grad_query, grad_output], 1) * factor, "dp", scatter_dimension=0, tiled=True
    )
    weight_grads = lax.psum(own_rows, "spatial")
    return (block_out, weight_grads)


def solution(mesh):
    return jax.shard_map(
        body,
        mesh=mesh,
        in_specs=(
            P("dp", "spatial", None, None),
            P("dp", "spatial", None),
            P(None, "dp", None),
            P(),
            P(None, "dp", None),
            P("dp", "spatial", None, None),
        ),
        out_specs=(P("dp", "spatial", None, None), P("dp", None, None)),
        check_vma=False,
    )
```

profile of v0, /device:TPU:1, one launch (start us, length us, event | category | flops | bytes accessed | tf_op | source)
XLA Modules:
  0.0 876.4 jit_solution(7868620939936180710)
XLA Ops:
  8.0 1.8 copy.29
  11.2 33.4 %all-reduce.2 = (f32[2,32]{1,0:T(2,128)S(1)}, f32[2,32]{1,0:T(2,128)S(1)}) all-reduce(f32[2,32]{1,0:T(2,128)S(1)} %reduce_sum.55, f32[2,32]{1,0:T(2,128)S(1)} %reduce_sum.52), channel_id=1, replica_groups=mesh['dp'=32,'spatial'=16] {'spatial'}, use_global_device_ids=true, to_apply=%region_5.6 | all-reduce | flops 128 | bytes 1024 | tf_op jit(solution)/shard_map/psum | solution.py:41
  45.2 1.9 collective-permute-start
  47.1 2.4 collective-permute-start.1
  49.5 19.2 %all_gather.10 = bf16[2,256,640]{2,1,0:T(8,128)(2,1)S(1)} all-gather(bf16[2,16,640]{2,1,0:T(8,128)(2,1)S(1)} %copy-done.7), channel_id=1, replica_groups=mesh['dp'=32,'spatial'=16] {'spatial'}, dimensions={1}, use_global_device_ids=true | all-gather | bytes 696320 | tf_op jit(solution)/shard_map/all_gather | solution.py:76
  75.1 89.4 %all-gather.5.cloned.1.call-done = bf16[4,640,640]{2,0,1:T(4,128)(2,1)} async-done(((bf16[4,20,640]{2,0,1:T(4,128)(2,1)}), bf16[4,640,640]{2,0,1:T(4,128)(2,1)}) %all-gather.5.cloned.1.call-update) | async-done | bytes 3276816 | tf_op jit(solution)/shard_map/all_gather | solution.py:70
  164.4 12.3 %fusion.57 = (bf16[1,640,640]{2,0,1:T(2,128)(2,1)S(1)}, bf16[1,640,640]{2,0,1:T(2,128)(2,1)S(1)}, bf16[1,640,640]{2,0,1:T(2,128)(2,1)}, bf16[1,640,640]{2,0,1:T(2,128)(2,1)}) fusion(bf16[4,640,640]{2,0,1:T(4,128)(2,1)} %all-gather.5.cloned.1.call-done), kind=kLoop, calls=%fused_computation.73 | loop fusion | bytes 6553600 | tf_op jit(solution)/shard_map/slice | solution.py:74
  176.7 1.6 convolution_convert_fusion
  180.7 2.2 convolution_convert_fusion.1
  184.0 1.4 fusion.33
  185.4 213.4 %all-gather.3.cloned.1.call-done = bf16[9,640,640]{2,0,1:T(8,128)(2,1)} async-done(((bf16[9,20,640]{2,0,1:T(8,128)(2,1)}), bf16[9,640,640]{2,0,1:T(8,128)(2,1)}) %all-gather.3.cloned.1.call-update) | async-done | bytes 7372816 | tf_op jit(solution)/shard_map/all_gather | solution.py:64
  398.8 7.7 fusion.27
  408.7 2.6 fusion.60
  411.3 2.5 fusion.19
  413.8 9.3 %fusion.20 = bf16[2,64,10,64]{1,3,2,0:T(8,128)(2,1)S(1)} fusion(f32[2,10,64,256]{3,2,1,0:T(8,128)} %fusion.33, bf16[2,256,10,64]{1,0,3,2:T(2,128)(2,1)S(1)} %copy-done.3, f32[2,10,64,256]{3,2,1,0:T(8,128)} %get-tuple-element.27, f32[2,10,64]{2,1,0:T(8,128)S(1)} %get-tuple-element.26), kind=kOutput, calls=%fused_computation.25 | convolution fusion | flops 44320256 | bytes 3445760 | tf_op jit(solution)/shard_map/bhnm,bmhe->bnhe/dot_general | solution.py:113
  424.3 1.4 convolution_bitcast_fusion.1
  425.7 2.0 copy.40
  427.7 1.8 convert_element_type.72
  431.2 4.3 copy.47
  435.6 1.3 dynamic-slice
  437.6 285.5 %all-reduce.8.cloned.1.call-done = f32[640,2,640]{2,1,0:T(2,128)} async-done(((f32[640,2,640]{2,1,0:T(2,128)}), f32[640,2,640]{2,1,0:T(2,128)}) %all-reduce.8.cloned.1.call-update) | async-done | bytes 3276816
  723.1 1.5 constant_dynamic-slice_fusion
  725.7 142.7 %all-reduce.6.cloned.1.call-done = f32[20,2,640]{2,1,0:T(2,128)} async-done(((f32[20,2,640]{2,1,0:T(2,128)}), f32[20,2,640]{2,1,0:T(2,128)}) %all-reduce.6.cloned.1.call-update) | async-done | bytes 102416 | tf_op jit(solution)/shard_map/psum | solution.py:123
  868.3 1.5 copy.107
  (65 shorter events, 18.6 us)
Async XLA Ops:
  7.2 176.2 %copy-start = (bf16[2,2,32,640]{3,2,1,0:T(8,128)(2,1)S(1)}, bf16[2,2,32,640]{3,2,1,0:T(8,128)(2,1)}, u32[]{:S(2)}) copy-start(bf16[2,2,32,640]{3,2,1,0:T(8,128)(2,1)} %param.11) | copy-start | bytes 491524
  7.2 37.8 %copy-start.4 = (bf16[2,2,32,640]{3,2,1,0:T(8,128)(2,1)S(1)}, bf16[2,2,32,640]{3,2,1,0:T(8,128)(2,1)}, u32[]{:S(2)}) copy-start(bf16[2,2,32,640]{3,2,1,0:T(8,128)(2,1)} %param.6) | copy-start | bytes 491524
  7.2 37.8 %copy-start.8 = (f32[640]{0:T(1024)S(1)}, f32[640]{0:T(1024)}, u32[]{:S(2)}) copy-start(f32[640]{0:T(1024)} %param.9) | copy-start | bytes 7684
  7.2 42.3 %copy-start.7 = (bf16[2,16,640]{2,1,0:T(8,128)(2,1)S(1)}, bf16[2,16,640]{2,1,0:T(8,128)(2,1)}, u32[]{:S(2)}) copy-start(bf16[2,16,640]{2,1,0:T(8,128)(2,1)} %param.7) | copy-start | bytes 122884
  7.2 157.2 %all-gather.5.cloned.1.call-start = ((), (), s32[]{:S(2)}) async-start(), calls=%async_computation.1 | async-start | bytes 3379200 | tf_op jit(solution)/shard_map/all_gather | solution.py:70
  7.9 390.9 %all-gather.3.cloned.1.call-start = ((), (), s32[]{:S(2)}) async-start(), calls=%async_computation | async-start | bytes 13516800 | tf_op jit(solution)/shard_map/all_gather | solution.py:64
  9.8 713.3 %all-reduce.8.cloned.1.call-start = ((), (), s32[]{:S(2)}) async-start(), calls=%async_computation.3 | async-start | bytes 6553600
  45.2 23.5 %collective-permute-start = (bf16[2,1,32,640]{3,2,1,0:T(8,128)(2,1)S(1)}, bf16[2,1,32,640]{3,2,1,0:T(8,128)(2,1)S(1)}, u32[]{:S(2)}, u32[]{:S(2)}) collective-permute-start(bf16[2,1,32,640]{3,2,1,0:T(8,128)(2,1)S(1)} %get-tuple-element.22), channel_id=1, source_target_pairs={{0,1},{1,2},{2,3},{3,4},{4,5},{5,6},{6,7},{7,8},{8,9},{9,10},{10,1... | collective-permute-start | bytes 245768 | tf_op jit(solution)/shard_map/ppermute | solution.py:23
  47.1 21.6 %collective-permute-start.1 = (bf16[2,1,32,640]{3,2,1,0:T(8,128)(2,1)S(1)}, bf16[2,1,32,640]{3,2,1,0:T(8,128)(2,1)S(1)}, u32[]{:S(2)}, u32[]{:S(2)}) collective-permute-start(bf16[2,1,32,640]{3,2,1,0:T(8,128)(2,1)S(1)} %get-tuple-element.23), channel_id=1, source_target_pairs={{1,0},{2,1},{3,2},{4,3},{5,4},{6,5},{7,6},{8,7},{9,8},{10,9},{11,1... | collective-permute-start | bytes 245768 | tf_op jit(solution)/shard_map/ppermute | solution.py:25
  398.8 8.4 copy-start.1
  406.6 0.7 copy-start.5
  406.6 2.1 copy-start.3
  435.5 289.1 %copy-start.2 = (bf16[128,640]{0,1:T(8,128)(2,1)S(1)}, bf16[128,640]{0,1:T(8,128)(2,1)}, u32[]{:S(2)}) copy-start(bf16[128,640]{0,1:T(8,128)(2,1)} %convert_element_type.72) | copy-start | bytes 491524
  435.5 289.1 %copy-start.6 = (bf16[128,640]{1,0:T(8,128)(2,1)S(1)}, bf16[128,640]{1,0:T(8,128)(2,1)}, u32[]{:S(2)}) copy-start(bf16[128,640]{1,0:T(8,128)(2,1)} %copy-done.5) | copy-start | bytes 491524
  435.5 432.8 %all-reduce.6.cloned.1.call-start = ((), (), s32[]{:S(2)}) async-start(), calls=%async_computation.2 | async-start | bytes 204800 | tf_op jit(solution)/shard_map/psum | solution.py:123
Sparse Core Ops, SparseCore 0:
  11.1 153.2 all-gather.4
  167.5 231.2 all-gather.2
  435.6 287.3 all-reduce.7
  726.4 141.8 all-reduce.5
where the time goes:
time: 877 us; the launch traced here: 876 us
  waiting for transfers between devices  732 us (83%)
  blocking collectives  52.6 us (6%)
  local copies, waits for them, and re-layouts  39.4 us (4%)
  matrix products  31.7 us (4%)
  between operations  14.7 us (2%)
    unnamed x5, waiting for transfers between devices  286 us
    all_gather x1, waiting for transfers between devices, body(): lax.all_gather(conv_weight, 'dp', axis=1, tiled=True)  213 us
    psum x1, waiting for transfers between devices, body(): weight_grads = lax.psum(own_rows, 'spatial')  143 us
    all_gather x1, waiting for transfers between devices, body(): weights = lax.all_gather(attn_weights, 'dp', axis=1, tiled=True)  89.4 us
    psum x1, blocking collectives, body(): first_sums, second_sums = lax.psum((first_sums, second_sums), 'spatial')  33.4 us
    all_gather x1, blocking collectives, body(): plan_all = lax.all_gather(plan, 'spatial', axis=1, tiled=True)  19.2 us
  transfers between devices with their start and end apart: 6, of which 4 were waited for; matrix products, arithmetic and copies ran while one was open for 4% of the time, Pallas kernels for 0%

commit v1 on v0

v1 whole, which is shorter than its diff:
```python
import math

import jax
import jax.numpy as jnp
from jax import lax
from jax.experimental import pallas as pl
from jax.experimental.pallas import tpu as pltpu
from jax.sharding import PartitionSpec as P

GROUPS = 32
HEAD = 64
NX = 4
NY = 4
QUAD = 4
MESH = pl.DeviceIdType.MESH
VMEM_LIMIT = 62 * 1024 * 1024

eps_norm = 1e-05


def wrap(value, n):
    return lax.rem(value + n, n)


class Spot:
    def __init__(self):
        self.nz = lax.axis_size("dp") // 2
        dp = lax.axis_index("dp")
        self.s = lax.axis_index("spatial")
        self.xh = lax.div(dp, self.nz)
        self.z = lax.rem(dp, self.nz)
        self.xl = lax.div(self.s, 2 * NY)
        self.y = lax.rem(lax.div(self.s, 2), NY)
        self.c = lax.rem(self.s, 2)
        self.x = 2 * self.xh + self.xl
        self.dp = dp

    def at(self, x=None, y=None, z=None, c=None):
        x = self.x if x is None else wrap(x, NX)
        y = self.y if y is None else wrap(y, NY)
        z = self.z if z is None else wrap(z, self.nz)
        c = self.c if c is None else c
        return (lax.div(x, 2) * self.nz + z, (lax.rem(x, 2) * NY + y) * 2 + c)

    def band(self, s):
        return (self.dp, s)


def send(src, dst, send_sem, recv_sem, device):
    pltpu.make_async_remote_copy(
        src_ref=src,
        dst_ref=dst,
        send_sem=send_sem,
        recv_sem=recv_sem,
        device_id=device,
        device_id_type=MESH,
    ).start()


def await_bytes(ref, sem):
    pltpu.make_async_copy(ref, ref, sem).wait()


def greet(spot, devices):
    barrier = pltpu.get_barrier_semaphore()
    for device in devices:
        pl.semaphore_signal(barrier, inc=1, device_id=device, device_id_type=MESH)
    pl.semaphore_wait(barrier, len(devices))


def gather_kernel(
    wslice, lat, plan, sums, cot, gain,
    block_out, ops,
    wmain, wext, zbuf, tmpf, stage, planb, halo, sbuf, taps, keys, vals, gatt,
    z_send, zr_recv, zl_recv, a_send, b_send, c_send, d_send, e_send, f_send,
    a_recv, b_recv, c_recv, d_recv, e_recv, f_recv,
    misc_send, misc_recv,
):
    me = Spot()
    nz, x, y, z, c, s = me.nz, me.x, me.y, me.z, me.c, me.s
    spatial = 4 * NY
    per_core = 2 * NY
    nq = nz // QUAD
    shard = 20
    unit = QUAD * shard
    half = nz * shard
    side = jnp.where(me.xl == 0, -1, 1)
    other_x = me.at(x=x + side)
    twin = me.at(c=1 - c)

    def sid(xx, yy):
        return c * per_core + lax.rem(wrap(xx, NX), 2) * NY + wrap(yy, NY)

    mates = [me.band(wrap(s + k, spatial)) for k in range(1, spatial)]
    greet(me, mates + [me.at(z=z + 1), me.at(z=z - 1), other_x])

    for k, mate in enumerate(mates):
        send(sums, sbuf.at[s], misc_send.at[0], misc_recv.at[0], mate)
    send(lat.at[:, 0], halo.at[1], misc_send.at[1], misc_recv.at[1], me.band(wrap(s - 1, spatial)))
    send(lat.at[:, 1], halo.at[0], misc_send.at[2], misc_recv.at[2], me.band(wrap(s + 1, spatial)))
    send(wslice, zbuf.at[z], z_send.at[0], zr_recv.at[0], me.at(z=z + 1))
    send(wslice, zbuf.at[z], z_send.at[1], zl_recv.at[0], me.at(z=z - 1))
    zbuf[z] = wslice[...]
    my_sid = sid(x, y)
    for dx in range(2):
        for dy in range(NY):
            if dx or dy:
                target = ((me.dp), (lax.rem(me.xl + dx, 2) * NY + wrap(y + dy, NY)) * 2 + c)
                send(plan, planb.at[:, my_sid], misc_send.at[3], misc_recv.at[3], target)
    planb[:, my_sid] = plan[...]
    sbuf[s] = sums[...]

    def z_step(k):
        await_bytes(zbuf.at[0], zr_recv.at[k - 1])
        if k < nz // 2:
            slot = wrap(z - k, nz)
            send(zbuf.at[slot], zbuf.at[slot], z_send.at[0], zr_recv.at[k], me.at(z=z + 1))
        if k < nz // 2:
            await_bytes(zbuf.at[0], zl_recv.at[k - 1])
            if k < nz // 2 - 1:
                slot = wrap(z + k, nz)
                send(zbuf.at[slot], zbuf.at[slot], z_send.at[1], zl_recv.at[k], me.at(z=z - 1))

    def block(xx, yy, q, colours=slice(None), dirs=slice(None)):
        row = pl.multiple_of(lax.div(wrap(xx, NX), 2) * half + q * unit, 16)
        return wmain.at[sid(xx, yy), colours, dirs, pl.ds(row, unit), :]

    def move(r, q, xx, yy, colours, dirs, send_sem, recv_sem, device):
        ref = block(xx, yy, q, colours, dirs)
        send(ref, ref, send_sem, recv_sem.at[r], device)

    every = slice(None)
    north, south = me.at(y=y + 1), me.at(y=y - 1)
    east, west = me.at(x=x + 1), me.at(x=x - 1)

    def part_a(r, q):
        for i in range(QUAD):
            tmpf[...] = zbuf[q * QUAD + i].astype(jnp.float32)
            for j in range(5):
                stage[j, i * shard:(i + 1) * shard, :] = tmpf[j * shard:(j + 1) * shard, :]
        row = pl.multiple_of(me.xh * half + q * unit, 16)
        for j in range(4):
            wmain[my_sid, j // 2, j % 2, pl.ds(row, unit), :] = stage[j].astype(jnp.bfloat16)
        wext[pl.ds(row, unit), :] = stage[4].astype(jnp.bfloat16)
        for device in (east, west, north, south):
            move(r, q, x, y, every, every, a_send, a_recv, device)
        send(wext.at[pl.ds(row, unit), :], wext.at[pl.ds(row, unit), :], e_send, e_recv, other_x)
        move(0, q, x, y, every, every, f_send, f_recv, twin)

    def part_b(r, q):
        await_bytes(wmain.at[pl.ds(0, 4), :, :, pl.ds(0, unit), :], a_recv.at[r])
        move(r, q, x - 1, y, every, pl.ds(0, 1), b_send, b_recv, east)
        move(r, q, x + 1, y, every, pl.ds(1, 1), b_send, b_recv, west)
        move(r, q, x, y - 1, every, pl.ds(0, 1), b_send, b_recv, north)
        move(r, q, x, y + 1, every, pl.ds(1, 1), b_send, b_recv, south)
        for k in (1, -1):
            for device in (north, south):
                move(r, q, x + k, y, pl.ds(0, 1), every, c_send, c_recv, device)
            for device in (east, west):
                move(r, q, x, y + k, pl.ds(1, 1), every, c_send, c_recv, device)
        for k in (1, -1):
            move(0, q, x + k, y, every, every, f_send, f_recv, twin)
            move(0, q, x, y + k, every, every, f_send, f_recv, twin)

    def part_c(r, q):
        await_bytes(wmain.at[pl.ds(0, 2), :, :, pl.ds(0, unit), :], b_recv.at[r])
        for device in (north, south):
            move(r, q, x + 2, y, pl.ds(0, 1), every, c_send, c_recv, device)
        for device in (east, west):
            move(r, q, x, y + 2, pl.ds(1, 1), every, c_send, c_recv, device)
        move(0, q, x + 2, y, every, every, f_send, f_recv, twin)
        move(0, q, x, y + 2, every, every, f_send, f_recv, twin)

    def part_d(r, q):
        await_bytes(wmain.at[pl.ds(0, 6), :, :, pl.ds(0, unit), :], c_recv.at[r])
        for k in (1, -1, 2):
            move(r, q, x + k, y - 1, pl.ds(0, 1), pl.ds(0, 1), d_send, d_recv, north)
            move(r, q, x + k, y + 1, pl.ds(0, 1), pl.ds(1, 1), d_send, d_recv, south)
            move(r, q, x - 1, y + k, pl.ds(1, 1), pl.ds(0, 1), d_send, d_recv, east)
            move(r, q, x + 1, y + k, pl.ds(1, 1), pl.ds(1, 1), d_send, d_recv, west)
        for i in (1, -1):
            for j in (1, -1):
                move(0, q, x + i, y + j, every, every, f_send, f_recv, twin)

    def part_e(r, q):
        await_bytes(wmain.at[pl.ds(0, 3), :, :, pl.ds(0, unit), :], d_recv.at[r])
        for i, j in ((1, 2), (-1, 2), (2, 1), (2, -1), (2, 2)):
            move(0, q, x + i, y + j, every, every, f_send, f_recv, twin)

    quad, inner = lax.div(z, QUAD), lax.rem(z, QUAD)
    near = jnp.where(inner < QUAD // 2, -1, 1)
    if nq == 4:
        rounds = [quad, wrap(quad + near, nq), wrap(quad - near, nq), wrap(quad + 2, nq)]
        steps = [3, 2, 2, 1]
    else:
        rounds, steps = [quad], [nz // 2]
    done = 0

    def steps_for(r):
        nonlocal done
        for _ in range(steps[r]):
            done += 1
            z_step(done)

    steps_for(0)
    part_a(0, rounds[0])
    await_bytes(planb.at[:, pl.ds(0, per_core - 1)], misc_recv.at[3])
    mine = planb.at[:, pl.ds(c * per_core, per_core)]
    send(mine, mine, misc_send.at[4], misc_recv.at[4], twin)
    await_bytes(sbuf.at[pl.ds(0, spatial - 1)], misc_recv.at[0])
    await_bytes(halo.at[0], misc_recv.at[1])
    await_bytes(halo.at[0], misc_recv.at[2])
    norm_taps(me, lat, gain, halo, sbuf, taps)
    for r in range(nq):
        if r + 1 < nq:
            steps_for(r + 1)
        part_b(r, rounds[r])
        part_c(r, rounds[r])
        if r + 1 < nq:
            part_a(r + 1, rounds[r + 1])
        if r:
            part_d(r - 1, rounds[r - 1])
        if r > 1:
            part_e(r - 2, rounds[r - 2])
    part_d(nq - 1, rounds[nq - 1])
    if nq > 1:
        part_e(nq - 2, rounds[nq - 2])
    part_e(nq - 1, rounds[nq - 1])

    await_bytes(planb.at[:, pl.ds(0, per_core)], misc_recv.at[4])
    await_bytes(wext.at[pl.ds(0, half)], e_recv)
    await_bytes(wmain.at[pl.ds(0, per_core)], f_recv.at[0])

    await_bytes(sbuf.at[pl.ds(0, spatial - 1)], misc_send.at[0])
    await_bytes(halo.at[0], misc_send.at[1])
    await_bytes(halo.at[0], misc_send.at[2])
    await_bytes(planb.at[:, pl.ds(0, per_core - 1)], misc_send.at[3])
    await_bytes(planb.at[:, pl.ds(0, per_core)], misc_send.at[4])
    await_bytes(zbuf.at[pl.ds(0, nz // 2)], z_send.at[0])
    await_bytes(zbuf.at[pl.ds(0, nz // 2 - 1)], z_send.at[1])
    await_bytes(wmain.at[pl.ds(0, 2)], a_send)
    await_bytes(wmain.at[pl.ds(0, 1)], b_send)
    await_bytes(wmain.at[pl.ds(0, 3)], c_send)
    await_bytes(wmain.at[pl.ds(0, 3), pl.ds(0, 1)], d_send)
    await_bytes(wext.at[pl.ds(0, half)], e_send)
    await_bytes(wmain.at[pl.ds(0, per_core)], f_send)

    plan_side(cot, planb, wmain, wext, keys, vals, gatt)
    convolve(lat, wmain, wext, taps, ops.at[0, 0])
    attend(
        ops.at[0, 0], wmain, wext, keys, vals, gatt, ops.at[1, 0], ops.at[0, 1], block_out
    )
    ops[1, 1] = cot[...].reshape(ops.shape[2:])


def gather_all(wslice, latents, plan, sums, cotangent, gain):
    nz = lax.axis_size("dp") // 2
    spatial = 4 * NY
    nq = nz // QUAD
    rows = 2 * nz * 20
    images, band_rows, columns, channels = latents.shape
    tokens = images * band_rows * columns
    plan_tokens = spatial * plan.shape[1]
    bf16, f32 = jnp.bfloat16, jnp.float32
    dma = pltpu.SemaphoreType.DMA
    return pl.pallas_call(
        gather_kernel,
        out_shape=[
            jax.ShapeDtypeStruct(latents.shape, bf16),
            jax.ShapeDtypeStruct((2, 2, tokens, channels), bf16),
        ],
        in_specs=[pl.BlockSpec(memory_space=pltpu.VMEM)] * 6,
        out_specs=[pl.BlockSpec(memory_space=pltpu.VMEM)] * 2,
        scratch_shapes=[
            pltpu.VMEM((spatial, 2, 2, rows, 128), bf16),
            pltpu.VMEM((rows, 128), bf16),
            pltpu.VMEM((nz, 112, 128), bf16),
            pltpu.VMEM((112, 128), f32),
            pltpu.VMEM((5, QUAD * 20, 128), f32),
            pltpu.VMEM((images, spatial) + plan.shape[1:], bf16),
            pltpu.VMEM((2, images, columns, channels), bf16),
            pltpu.VMEM((spatial, 8, channels), f32),
            pltpu.VMEM((3, images, band_rows + 2, columns, channels), bf16),
            pltpu.VMEM((images, plan_tokens, channels), bf16),
            pltpu.VMEM((images, plan_tokens, channels), bf16),
            pltpu.VMEM((tokens, channels), bf16),
            dma((2,)), dma((nz // 2,)), dma((nz // 2,)),
            dma, dma, dma, dma, dma, dma,
            dma((nq,)), dma((nq,)), dma((nq,)), dma((nq,)), dma, dma((1,)),
            dma((5,)), dma((5,)),
        ],
        compiler_params=pltpu.CompilerParams(
            collective_id=0, has_side_effects=True, vmem_limit_bytes=VMEM_LIMIT
        ),
        name="gather_all",
    )(wslice, latents, plan, sums, cotangent, gain)


def column_block(wmain, wext, index):
    if index < 64:
        return wmain[index // 4, index % 4 // 2, index % 2]
    return wext[...]


def columns_of(wmain, wext, matrix, start, stop):
    parts = [column_block(wmain, wext, 5 * matrix + n) for n in range(start, stop)]
    return parts[0] if len(parts) == 1 else jnp.concatenate(parts, axis=1)


SPANS = ((0, 2), (2, 4), (4, 5))


def norm_taps(me, lat, gain, halo, sbuf, taps):
    images, band_rows, columns, channels = lat.shape
    spatial = 4 * NY
    f32 = jnp.float32
    tot = sbuf[0]
    for i in range(1, spatial):
        tot = tot + sbuf[i]
    wide = channels // GROUPS
    one = lax.broadcasted_iota(jnp.int32, (channels, channels), 0).astype(f32)
    two = lax.broadcasted_iota(jnp.int32, (channels, channels), 1).astype(f32)
    same = jnp.floor((one + 0.5) * (1.0 / wide)) == jnp.floor((two + 0.5) * (1.0 / wide))
    grouped = jnp.dot(
        tot, same.astype(f32), preferred_element_type=f32, precision=lax.Precision.HIGHEST
    )
    counted = float(band_rows * spatial * columns * wide)
    row_at = lax.broadcasted_iota(jnp.int32, (columns, channels), 0)
    for i in range(images):
        mean = grouped[i:i + 1] / counted
        variance = grouped[images + i:images + i + 1] / counted - mean * mean
        inverse = lax.rsqrt(variance + eps_norm)
        for r in range(band_rows + 2):
            if r == 0:
                cells = halo[0, i]
            elif r == band_rows + 1:
                cells = halo[1, i]
            else:
                cells = lat[i, r - 1]
            normed = (cells.astype(f32) - mean) * inverse * gain[...]
            hidden = (normed / (1.0 + jnp.exp(-normed))).astype(jnp.bfloat16).astype(f32)
            if r == 0:
                hidden = jnp.where(me.s == 0, 0.0, hidden)
            if r == band_rows + 1:
                hidden = jnp.where(me.s == spatial - 1, 0.0, hidden)
            before = jnp.where(row_at == 0, 0.0, pltpu.roll(hidden, 1, 0))
            after = jnp.where(row_at == columns - 1, 0.0, pltpu.roll(hidden, columns - 1, 0))
            taps[0, i, r] = before.astype(jnp.bfloat16)
            taps[1, i, r] = hidden.astype(jnp.bfloat16)
            taps[2, i, r] = after.astype(jnp.bfloat16)


def plan_side(cot, planb, wmain, wext, keys, vals, gatt):
    images, spatial, plan_rows, channels = planb.shape
    f32, bf16 = jnp.float32, jnp.bfloat16
    for start, stop in SPANS:
        lanes = slice(128 * start, 128 * stop)
        weight_k = columns_of(wmain, wext, 10, start, stop)
        weight_v = columns_of(wmain, wext, 11, start, stop)
        for i in range(images):
            rows = planb[i].reshape(spatial * plan_rows, channels)
            keys[i, :, lanes] = jnp.dot(rows, weight_k, preferred_element_type=f32).astype(bf16)
            vals[i, :, lanes] = jnp.dot(rows, weight_v, preferred_element_type=f32).astype(bf16)
    total = None
    flat = cot[...].reshape(-1, channels)
    for start, stop in SPANS:
        weight_o = columns_of(wmain, wext, 12, start, stop)
        part = lax.dot_general(
            flat[:, 128 * start:128 * stop], weight_o, (((1,), (1,)), ((), ())),
            preferred_element_type=f32,
        )
        total = part if total is None else total + part
    gatt[...] = total.astype(bf16)


def convolve(lat, wmain, wext, taps, mixed):
    images, band_rows, columns, channels = lat.shape
    tokens = images * band_rows * columns
    flat = lat[...].reshape(tokens, channels)
    for start, stop in SPANS:
        lanes = slice(128 * start, 128 * stop)
        total = None
        for t in range(9):
            window = taps[t % 3, :, t // 3:t // 3 + band_rows].reshape(tokens, channels)
            part = jnp.dot(
                window, columns_of(wmain, wext, t, start, stop), preferred_element_type=jnp.float32
            )
            total = part if total is None else total + part
        mixed[:, lanes] = (flat[:, lanes].astype(jnp.float32) + total).astype(jnp.bfloat16)


def attend(mixed, wmain, wext, keys, vals, gatt, attended, dquery, block_out):
    images, band_rows, columns, channels = block_out.shape
    f32, bf16 = jnp.float32, jnp.bfloat16
    scale = 1.0 / math.sqrt(HEAD)
    cells = band_rows * columns
    tokens = images * cells
    nt = (((1,), (1,)), ((), ()))
    left = lax.broadcasted_iota(jnp.int32, (cells, 128), 1) < HEAD
    zero = jnp.zeros((cells, 128), bf16)

    def two_heads(value):
        return jnp.concatenate([jnp.where(left, value, zero), jnp.where(left, zero, value)], 0)

    def one_row(value):
        return jnp.where(left, value[:cells], value[cells:]).astype(bf16)

    flat = mixed[...]
    for start, stop in SPANS:
        queries = jnp.dot(
            flat, columns_of(wmain, wext, 9, start, stop), preferred_element_type=f32
        ).astype(bf16)
        for n in range(start, stop):
            lanes = slice(128 * n, 128 * n + 128)
            here = slice(128 * (n - start), 128 * (n - start) + 128)
            for i in range(images):
                rows = slice(cells * i, cells * i + cells)
                key, val = keys[i, :, lanes], vals[i, :, lanes]
                query = two_heads(queries[rows, here])
                grad = two_heads(gatt[rows, lanes])
                scores = lax.dot_general(query, key, nt, preferred_element_type=f32) * scale
                expo = jnp.exp(scores - jnp.max(scores, axis=-1, keepdims=True))
                probs = expo / jnp.sum(expo, axis=-1, keepdims=True)
                dprob = lax.dot_general(grad, val, nt, preferred_element_type=f32)
                inner = jnp.sum(probs * dprob, axis=-1, keepdims=True)
                dscore = (probs * (dprob - inner) * scale).astype(bf16)
                attended[rows, lanes] = one_row(
                    jnp.dot(probs.astype(bf16), val, preferred_element_type=f32)
                )
                dquery[rows, lanes] = one_row(jnp.dot(dscore, key, preferred_element_type=f32))
    for start, stop in SPANS:
        lanes = slice(128 * start, 128 * stop)
        result = flat[:, lanes].astype(f32) + jnp.dot(
            attended[...], columns_of(wmain, wext, 12, start, stop), preferred_element_type=f32
        )
        block_out[:, :, :, lanes] = result.astype(bf16).reshape(
            images, band_rows, columns, 128 * (stop - start)
        )


def reduce_kernel(
    factor,
    ops, perm,
    out,
    rcv, gf, gb, r1, h, r2, total, zs, zr, fin,
    op_sems, s1_send, s1_recv, s2_send, s2_recv, z_sems, o_sems,
):
    me = Spot()
    nz, x, y, z, c, s = me.nz, me.x, me.y, me.z, me.c, me.s
    spatial = 4 * NY
    zh = nz // 2
    small = zh * 5
    big = 4 * small
    twin = me.at(c=1 - c)
    mates = [me.band(wrap(s + k, spatial)) for k in range(1, spatial)]
    away = jnp.where(me.xl == 0, -1, 1)
    greet(
        me,
        mates + [me.at(z=z + k) for k in range(1, nz)] + [me.at(x=x + away), me.at(x=x + 2)],
    )
    send(ops.at[1 - c], rcv, op_sems.at[0], op_sems.at[1], twin)
    own = ops[c]
    await_bytes(rcv, op_sems.at[1])
    lhs = jnp.concatenate([own[0], rcv[0]], axis=0)
    rhs = jnp.concatenate([own[1], rcv[1]], axis=0)
    lhs = jnp.dot(lhs, perm[...], preferred_element_type=jnp.float32).astype(jnp.bfloat16)
    grads = lax.dot_general(
        lhs, rhs, (((0,), (0,)), ((), ())), preferred_element_type=jnp.float32
    ) * factor
    gf[...] = grads
    gb[...] = grads.astype(jnp.bfloat16)
    first = c == 0
    a1 = jnp.where(first, y, x)
    a2 = jnp.where(first, x, y)
    for k in (2, 1, 3):
        to = wrap(a1 + k, 4)
        device = me.at(x=jnp.where(first, x, to), y=jnp.where(first, to, y))
        send(
            gb.at[pl.ds(pl.multiple_of(to * big, 32), big)],
            r1.at[k - 1], s1_send.at[k - 1], s1_recv.at[k - 1], device,
        )
    acc = gf[pl.ds(pl.multiple_of(a1 * big, 32), big)]
    for k in (1, 3, 2):
        await_bytes(r1.at[k - 1], s1_recv.at[k - 1])
        acc = acc + r1[k - 1].astype(jnp.float32)
    h[...] = acc
    for k in (2, 1, 3):
        to = wrap(a2 + k, 4)
        device = me.at(x=jnp.where(first, to, x), y=jnp.where(first, y, to))
        send(
            h.at[pl.ds(pl.multiple_of(to * small, 8), small)],
            r2.at[k - 1], s2_send.at[k - 1], s2_recv.at[k - 1], device,
        )
    acc = h[pl.ds(pl.multiple_of(a2 * small, 8), small)]
    for k in (1, 3, 2):
        await_bytes(r2.at[k - 1], s2_recv.at[k - 1])
        acc = acc + r2[k - 1]
    total[...] = acc
    zs[...] = jnp.zeros_like(zs)
    for i in range(zh):
        zs[i, 0:5, :] = total[5 * i:5 * i + 5, :]
    for i in range(zh):
        to = me.xl * zh + i

        @pl.when(to != z)
        def _():
            send(zs.at[i], zr.at[z], z_sems.at[0], z_sems.at[1], me.at(z=to))

    active = lax.div(z, zh) == me.xl

    @pl.when(active)
    def _():
        zr[z] = zs[z - me.xl * zh]
        await_bytes(zr.at[pl.ds(0, nz - 1)], z_sems.at[1])
        piece = zr[0]
        for i in range(1, nz):
            piece = piece + zr[i]
        fin[...] = piece
        for mate in mates:
            send(fin, out.at[c * NY + y], o_sems.at[0], o_sems.at[1], mate)
        out[c * NY + y] = piece
        await_bytes(out.at[pl.ds(0, 2 * NY - 1)], o_sems.at[1])
        await_bytes(zr.at[pl.ds(0, spatial - 1)], o_sems.at[0])
        await_bytes(zs.at[pl.ds(0, zh - 1)], z_sems.at[0])

    @pl.when(jnp.logical_not(active))
    def _():
        await_bytes(out, o_sems.at[1])
        await_bytes(zs, z_sems.at[0])

    await_bytes(rcv, op_sems.at[0])
    for k in range(3):
        await_bytes(r1.at[k], s1_send.at[k])
        await_bytes(r2.at[k], s2_send.at[k])


def reduce_all(ops, factor):
    nz = lax.axis_size("dp") // 2
    me = Spot()
    spatial = 4 * NY
    zh = nz // 2
    small, big = 5 * zh, 20 * zh
    rows, columns = ops.shape[-1], ops.shape[-1]
    used = 8 * big // 2
    natural = jnp.arange(rows)
    xx = natural // (20 * zh)
    yy = natural % 20 // 5
    place = jnp.where(me.c == 0, yy * 4 + xx, xx * 4 + yy) * small
    place = place + natural // 20 % zh * 5 + natural % 5
    perm = (place[:, None] == jnp.arange(used)[None, :]).astype(jnp.bfloat16)
    bf16, f32 = jnp.bfloat16, jnp.float32
    dma = pltpu.SemaphoreType.DMA
    import functools

    pieces = pl.pallas_call(
        functools.partial(reduce_kernel, factor),
        out_shape=jax.ShapeDtypeStruct((2 * NY, 8, columns), f32),
        in_specs=[pl.BlockSpec(memory_space=pltpu.VMEM)] * 2,
        out_specs=pl.BlockSpec(memory_space=pltpu.VMEM),
        scratch_shapes=[
            pltpu.VMEM(ops.shape[1:], bf16),
            pltpu.VMEM((used, columns), f32),
            pltpu.VMEM((used, columns), bf16),
            pltpu.VMEM((3, big, columns), bf16),
            pltpu.VMEM((big, columns), f32),
            pltpu.VMEM((3, small, columns), f32),
            pltpu.VMEM((small, columns), f32),
            pltpu.VMEM((zh, 8, columns), f32),
            pltpu.VMEM((max(nz, spatial), 8, columns), f32),
            pltpu.VMEM((8, columns), f32),
            dma((2,)), dma((3,)), dma((3,)), dma((3,)), dma((3,)), dma((2,)), dma((2,)),
        ],
        compiler_params=pltpu.CompilerParams(
            collective_id=1, has_side_effects=True, vmem_limit_bytes=VMEM_LIMIT
        ),
        name="reduce_all",
    )(ops, perm)
    pieces = pieces.reshape(2, NY, 8, columns)[:, :, :5]
    return pieces.transpose(1, 2, 0, 3).reshape(20, 2, columns)


def weight_slice(conv_weight, attn_weights):
    me = Spot()
    taps = conv_weight.shape[0] + attn_weights.shape[0]
    rows, channels = conv_weight.shape[1:]
    shard = jnp.concatenate([conv_weight, attn_weights], 0)
    shard = shard.reshape(taps, rows, channels // 128, 128).transpose(0, 2, 1, 3)
    shard = shard.reshape(-1, rows, 128)
    first = 4 * (me.c * 2 * NY + me.xl * NY + me.y)
    own = lax.dynamic_slice_in_dim(shard, first, 4, 0)
    own = jnp.concatenate([own, shard[-1:]], 0).reshape(-1, 128)
    return jnp.pad(own, ((0, 12), (0, 0)))


def body(latents, plan, conv_weight, gn_gain, attn_weights, cotangent):
    images, band_rows, columns, channels = latents.shape
    flat = latents.astype(jnp.float32).reshape(images, band_rows * columns, channels)
    sums = jnp.concatenate(
        [jnp.sum(flat, 1), jnp.sum(flat * flat, 1), jnp.zeros((8 - 2 * images, channels))], 0
    )
    block_out, ops = gather_all(
        weight_slice(conv_weight, attn_weights), latents, plan, sums, cotangent, gn_gain[None]
    )
    cells = images * band_rows * columns
    factor = 1.0 / math.sqrt(cells * lax.axis_size("dp") * lax.axis_size("spatial"))
    return (block_out, reduce_all(ops, factor))


def solution(mesh):
    return jax.shard_map(
        body,
        mesh=mesh,
        in_specs=(
            P("dp", "spatial", None, None),
            P("dp", "spatial", None),
            P(None, "dp", None),
            P(),
            P(None, "dp", None),
            P("dp", "spatial", None, None),
        ),
        out_specs=(P("dp", "spatial", None, None), P("dp", None, None)),
        check_vma=False,
    )
```

time: 877 us -> 132 us (0.15)
  waiting for transfers between devices: 732 us -> 0 us
  Pallas kernels: 0 us -> 121 us
  blocking collectives: 52.6 us -> 0 us
  local copies, waits for them, and re-layouts: 39.4 us -> 5.94 us
  matrix products: 31.7 us -> 0 us
  between operations: 14.7 us -> 0.76 us
    all_gather x2 -> x0, waiting for transfers between devices: 303 us -> none  [the longest x1 213 us: body(): lax.all_gather(conv_weight, 'dp', axis=1, tiled=True)]
    unnamed x5 -> x0, waiting for transfers between devices: 286 us -> none
    psum x1 -> x0, waiting for transfers between devices: 143 us -> none  [body(): weight_grads = lax.psum(own_rows, 'spatial')]
    pallas_call x0 -> x2, Pallas kernels: none -> 121 us  [the longest x1 80.4 us: gather_all(): pl.pallas_call(gather_kernel, out_shape=[jax.ShapeDtypeStruct(latents.sha...]
    psum x1 -> x0, blocking collectives: 33.4 us -> none  [body(): first_sums, second_sums = lax.psum((first_sums, second_sums), 'spatial')]
    dot_general x11 -> x0, matrix products: 29.1 us -> none  [the longest x1 9.33 us: body(): jnp.einsum('bhnm,bmhe->bnhe', dscore, key_heads, preferred_element_type=j...]
    all_gather x1 -> x0, blocking collectives: 19.2 us -> none  [body(): plan_all = lax.all_gather(plan, 'spatial', axis=1, tiled=True)]
    slice x3 -> x1, local copies, waits for them, and re-layouts: 12.4 us -> 0.01 us  [weight_slice(): own = jnp.concatenate([own, shard[-1:]], 0).reshape(-1, 128)]
  transfers between devices with their start and end apart: 6 -> 0, of which waited for: 4 -> 0; matrix products, arithmetic and copies ran while one was open for 4% -> 0% of each run, Pallas kernels for 0% -> 0%
where the time goes in v1:
time: 132 us; the launch traced here: 130 us
  Pallas kernels  121 us (92%)
  local copies, waits for them, and re-layouts  5.94 us (4%)
  other arithmetic  2.79 us (2%)
    pallas_call x1, Pallas kernels, gather_all(): pl.pallas_call(gather_kernel, out_shape=[jax.ShapeDtypeStruct(latents.sha...  80.4 us
    pallas_call x1, Pallas kernels, reduce_all(): pl.pallas_call(functools.partial(reduce_kernel, factor), out_shape=jax.Sh...  40.5 us

profile of v1, /device:TPU:1, one launch (start us, length us, event | category | flops | bytes accessed | tf_op | source)
XLA Modules:
  0.0 130.3 jit_solution(8148318603353748583)
XLA Ops:
  0.6 0.0 copy-start.1
  0.7 0.1 pad.7.clone
  0.7 1.3 broadcast_in_dim.9.gain
  2.1 1.0 convert_reduce_fusion
  3.0 0.7 maximum_maximum_fusion.sums
  3.7 1.0 constant_dynamic-update-slice_fusion
  4.7 0.0 copy-done.1
  4.7 0.1 fusion.24
  4.8 0.5 concatenate.13
  5.3 0.1 reshape.78
  5.4 0.6 pad.4.wslice
  6.1 80.4 %gather_all.1 = (bf16[2,2,32,640]{3,2,1,0:T(8,128)(2,1)}, bf16[2,2,128,640]{3,2,1,0:T(8,128)(2,1)}) custom-call(bf16[112,128]{1,0:T(8,128)(2,1)} %pad.4.wslice, bf16[2,2,32,640]{3,2,1,0:T(8,128)(2,1)} %lat.1, bf16[2,16,640]{2,1,0:T(8,128)(2,1)} %plan.1, f32[8,640]{1,0:T(8,128)} %maximum_maximum_fusion.sums, bf16[2,2,32,640]{3,2,1,0:T(8,128)(2,1)} %cot.1, ...), custom_call_target="tpu_custom_call" | custom-call | tf_op jit(solution)/shard_map/gather_all/pallas_call | solution.py:266
  86.4 1.1 fusion.perm
  87.5 0.0 copy-start
  87.5 40.5 %reduce_all.1 = f32[8,8,640]{2,1,0:T(8,128)} custom-call(bf16[2,2,128,640]{3,2,1,0:T(8,128)(2,1)} %get-tuple-element.5.ops, bf16[640,640]{1,0:T(8,128)(2,1)} %fusion.perm), custom_call_target="tpu_custom_call" | custom-call | tf_op jit(solution)/shard_map/reduce_all/pallas_call | solution.py:555
  128.0 0.9 slice_bitcast_fusion
  128.9 0.7 copy.11
  129.6 0.0 copy-done
  129.6 0.7 copy.15
  (7 shorter events, 0.1 us)
Async XLA Ops:
  0.6 4.1 %copy-start.1 = (bf16[4,20,640]{2,0,1:T(4,128)(2,1)S(1)}, bf16[4,20,640]{2,0,1:T(4,128)(2,1)}, u32[]{:S(2)}) copy-start(bf16[4,20,640]{2,0,1:T(4,128)(2,1)} %param.10) | copy-start | bytes 307204
  87.5 42.1 %copy-start = (bf16[2,2,32,640]{3,2,1,0:T(8,128)(2,1)S(1)}, bf16[2,2,32,640]{3,2,1,0:T(8,128)(2,1)}, u32[]{:S(2)}) copy-start(bf16[2,2,32,640]{3,2,1,0:T(8,128)(2,1)} %get-tuple-element.15) | copy-start | bytes 491524

commit v2 on v0

v2 whole, which is shorter than its diff:
```python
import functools
import math

import jax
import jax.numpy as jnp
from jax import lax
from jax.experimental import pallas as pl
from jax.experimental.pallas import tpu as pltpu
from jax.sharding import PartitionSpec as P

GROUPS = 32
HEAD = 64
NX = 4
NY = 4
BANDS = 16
CORE = 2 * NY
SHARD = 20
UNIT = 4 * SHARD
MESH = pl.DeviceIdType.MESH
VMEM_LIMIT = 62 * 1024 * 1024
SPANS = ((0, 2), (2, 4), (4, 5))
BF16 = jnp.bfloat16
F32 = jnp.float32
NT = (((1,), (1,)), ((), ()))

eps_norm = 1e-05


def wrap(value, n):
    return lax.rem(value + n, n)


class Spot:
    def __init__(self, nz):
        self.nz = nz
        self.dp = lax.axis_index("dp")
        self.s = lax.axis_index("spatial")
        self.xh = lax.div(self.dp, nz)
        self.z = lax.rem(self.dp, nz)
        self.xl = lax.div(self.s, CORE)
        self.y = lax.rem(lax.div(self.s, 2), NY)
        self.c = lax.rem(self.s, 2)
        self.x = 2 * self.xh + self.xl

    def at(self, x=None, y=None, z=None, c=None):
        x = self.x if x is None else wrap(x, NX)
        y = self.y if y is None else wrap(y, NY)
        z = self.z if z is None else wrap(z, self.nz)
        c = self.c if c is None else c
        return (lax.div(x, 2) * self.nz + z, (lax.rem(x, 2) * NY + y) * 2 + c)

    def sid(self, x, y):
        return self.c * CORE + lax.rem(wrap(x, NX), 2) * NY + wrap(y, NY)


def send(src, dst, send_sem, recv_sem, device):
    pltpu.make_async_remote_copy(
        src_ref=src,
        dst_ref=dst,
        send_sem=send_sem,
        recv_sem=recv_sem,
        device_id=device,
        device_id_type=MESH,
    ).start()


def await_bytes(ref, sem):
    pltpu.make_async_copy(ref, ref, sem).wait()


def reach(nz):
    steps = [0]
    for k in range(1, nz // 2):
        steps += [k, -k]
    return steps + [nz // 2]


def ints(shape, axis):
    return lax.broadcasted_iota(jnp.int32, shape, axis)


def floor_of(values, width):
    return jnp.floor((values + 0.5) * (1.0 / width))


def one_hot(names, rows):
    at = ints((rows, names.shape[1]), 0).astype(F32)
    return jnp.where(at == names, 1.0, 0.0).astype(BF16)


def arrival_order(me, channels):
    nz = me.nz
    bits = nz.bit_length() - 1
    place = ints((1, channels), 1)
    head = 2 * nz * 16
    late = place - head
    main = place < head
    slot = jnp.where(main, place >> 4, late >> 2)
    row = jnp.where(main, place & 15, 16 + (late & 3))
    half, slot = slot >> bits, slot & (nz - 1)
    step = jnp.where((slot & 1) == 1, (slot + 1) >> 1, -(slot >> 1))
    names = (half * nz + ((me.z + step + nz) & (nz - 1))) * SHARD + row
    return one_hot(names.astype(F32), channels)


def scatter_order(me, channels):
    zh = me.nz // 2
    small = 5 * zh
    place = ints((1, channels), 1).astype(F32)
    outer = floor_of(place, 4 * small)
    place = place - outer * (4 * small)
    inner = floor_of(place, small)
    place = place - inner * small
    zi = floor_of(place, 5)
    i = place - 5 * zi
    first = me.c == 0
    xx = jnp.where(first, inner, outer)
    yy = jnp.where(first, outer, inner)
    names = (xx * zh + zi) * SHARD + yy * 5 + i
    return one_hot(names, channels)


def group_table(channels):
    rows = ints((channels, 128), 0).astype(F32)
    lanes = ints((channels, 128), 1).astype(F32)
    return jnp.where(floor_of(rows, channels // GROUPS) == lanes, 1.0, 0.0)


def own_slice(me, conv, attn, wslice, extra, spare):
    taps, _, channels = conv.shape
    per = channels // 128
    first = 4 * me.sid(me.x, me.y)
    for j in range(4):
        block = first + j
        matrix = lax.div(block, per)
        lanes = pl.ds(pl.multiple_of(lax.rem(block, per) * 128, 128), 128)
        one = conv[jnp.minimum(matrix, taps - 1), :, lanes].astype(F32)
        two = attn[jnp.maximum(matrix - taps, 0), :, lanes].astype(F32)
        rows = jnp.where(matrix < taps, one, two)
        wslice[16 * j:16 * j + 16, :] = rows[0:16].astype(BF16)
        spare[4 * j:4 * j + 4, :] = rows[16:20]
    wslice[64:80, :] = spare[...].astype(BF16)
    extra[0:20, :] = attn[attn.shape[0] - 1, :, channels - 128:channels]
    extra[20:32, :] = jnp.zeros((12, 128), BF16)


def band_sums(lat, table, sums):
    images, band_rows, columns, channels = lat.shape
    rows = []
    for power in (1, 2):
        for i in range(images):
            cells = lat[i].reshape(band_rows * columns, channels).astype(F32)
            rows.append(jnp.sum(cells * cells if power == 2 else cells, axis=0, keepdims=True))
    rows.append(jnp.zeros((8 - 2 * images, channels), F32))
    sums[...] = jnp.dot(
        jnp.concatenate(rows, axis=0), table,
        preferred_element_type=F32, precision=lax.Precision.HIGHEST,
    )


def norm_taps(me, lat, gain, halo, sbuf, order, taps):
    images, band_rows, columns, channels = lat.shape
    tot = sbuf[0]
    for i in range(1, BANDS):
        tot = tot + sbuf[i]
    grouped = lax.dot_general(
        tot, group_table(channels), NT, preferred_element_type=F32, precision=lax.Precision.HIGHEST
    )
    counted = float(band_rows * BANDS * columns * (channels // GROUPS))
    row_at = ints((columns, channels), 0)
    for i in range(images):
        mean = grouped[i:i + 1] / counted
        variance = grouped[images + i:images + i + 1] / counted - mean * mean
        inverse = lax.rsqrt(variance + eps_norm)
        for r in range(band_rows + 2):
            if r == 0:
                cells = halo[0, i]
            elif r == band_rows + 1:
                cells = halo[1, i]
            else:
                cells = lat[i, r - 1]
            normed = (cells.astype(F32) - mean) * inverse * gain[...]
            hidden = (normed / (1.0 + jnp.exp(-normed))).astype(BF16)
            hidden = jnp.dot(hidden, order[...], preferred_element_type=F32)
            if r == 0:
                hidden = jnp.where(me.s == 0, 0.0, hidden)
            if r == band_rows + 1:
                hidden = jnp.where(me.s == BANDS - 1, 0.0, hidden)
            before = jnp.where(row_at == 0, 0.0, pltpu.roll(hidden, 1, 0))
            after = jnp.where(row_at == columns - 1, 0.0, pltpu.roll(hidden, columns - 1, 0))
            taps[0, i, r] = before.astype(BF16)
            taps[1, i, r] = hidden.astype(BF16)
            taps[2, i, r] = after.astype(BF16)


class Weights:
    def __init__(self, wmain, wext, wleft):
        self.wmain, self.wext, self.wleft = wmain, wext, wleft

    def gather_left(self):
        wmain, wext, wleft = self.wmain, self.wext, self.wleft
        count = wmain.shape[1] * wmain.shape[2] * 4
        low = ints((count // 2, 8, 128), 1) < 4

        def paired(tile):
            tile = tile.reshape(count // 2, 2, 8, 128)
            even, odd = tile[:, 0], tile[:, 1]
            first = jnp.where(low, even, pltpu.roll(odd, 4, 1))
            second = jnp.where(low, pltpu.roll(even, 4, 1), odd)
            return [v.reshape(count * 4, 128).astype(BF16) for v in (first, second)]

        def step(sid, carry):
            tile = wmain[sid, :, :, :, :, 64:80, :].reshape(count, 16, 128).astype(F32)
            for part in range(2):
                first, second = paired(tile[:, 8 * part:8 * part + 8])
                wleft[4 * sid + 2 * part] = first
                wleft[4 * sid + 2 * part + 1] = second
            return carry

        lax.fori_loop(0, wmain.shape[0], step, 0)
        tile = wext[:, :, 16:32, :].reshape(count, 16, 128).astype(F32)
        wleft[4 * wmain.shape[0]] = paired(tile[:, 0:8])[0]

    def block(self, index):
        wmain, wext = self.wmain, self.wext
        if index < 4 * wmain.shape[0]:
            j = index % 4
            head = wmain[index // 4, :, :, :, :, 16 * j:16 * j + 16, :]
        else:
            head = wext[:, :, 0:16, :]
        return jnp.concatenate([head.reshape(-1, 128), self.wleft[index]], axis=0)

    def columns(self, matrix, start, stop):
        parts = [self.block(5 * matrix + n) for n in range(start, stop)]
        return parts[0] if len(parts) == 1 else jnp.concatenate(parts, axis=1)


def order_plan(planb, order):
    images, bands, plan_rows, channels = planb.shape
    for i in range(images):
        rows = planb[i].reshape(bands * plan_rows, channels)
        rows = jnp.dot(rows, order[...], preferred_element_type=F32).astype(BF16)
        planb[i] = rows.reshape(bands, plan_rows, channels)


def plan_side(cot, planb, weights, order, keys, vals, gatt):
    images, bands, plan_rows, channels = planb.shape
    for start, stop in SPANS:
        lanes = slice(128 * start, 128 * stop)
        weight_k = weights.columns(10, start, stop)
        weight_v = weights.columns(11, start, stop)
        for i in range(images):
            rows = planb[i].reshape(bands * plan_rows, channels)
            keys[i, :, lanes] = jnp.dot(rows, weight_k, preferred_element_type=F32).astype(BF16)
            vals[i, :, lanes] = jnp.dot(rows, weight_v, preferred_element_type=F32).astype(BF16)
    total = None
    flat = cot[...].reshape(-1, channels)
    for start, stop in SPANS:
        part = lax.dot_general(
            flat[:, 128 * start:128 * stop], weights.columns(12, start, stop), NT,
            preferred_element_type=F32,
        )
        total = part if total is None else total + part
    total = lax.dot_general(total.astype(BF16), order[...], NT, preferred_element_type=F32)
    gatt[...] = total.astype(BF16)


def convolve(lat, weights, taps, mixed):
    images, band_rows, columns, channels = lat.shape
    tokens = images * band_rows * columns
    flat = lat[...].reshape(tokens, channels)
    for start, stop in SPANS:
        lanes = slice(128 * start, 128 * stop)
        total = None
        for t in range(9):
            window = taps[t % 3, :, t // 3:t // 3 + band_rows].reshape(tokens, channels)
            part = jnp.dot(window, weights.columns(t, start, stop), preferred_element_type=F32)
            total = part if total is None else total + part
        mixed[:, lanes] = (flat[:, lanes].astype(F32) + total).astype(BF16)


def attend(mixed, weights, order, keys, vals, gatt, attended, dquery, block_out):
    images, band_rows, columns, channels = block_out.shape
    scale = 1.0 / math.sqrt(HEAD)
    cells = band_rows * columns
    left = ints((cells, 128), 1) < HEAD
    zero = jnp.zeros((cells, 128), BF16)

    def two_heads(value):
        return jnp.concatenate([jnp.where(left, value, zero), jnp.where(left, zero, value)], 0)

    def one_row(value):
        return jnp.where(left, value[:cells], value[cells:]).astype(BF16)

    flat = mixed[...]
    ordered = jnp.dot(flat, order[...], preferred_element_type=F32).astype(BF16)
    for start, stop in SPANS:
        queries = jnp.dot(
            ordered, weights.columns(9, start, stop), preferred_element_type=F32
        ).astype(BF16)
        for n in range(start, stop):
            lanes = slice(128 * n, 128 * n + 128)
            here = slice(128 * (n - start), 128 * (n - start) + 128)
            for i in range(images):
                rows = slice(cells * i, cells * i + cells)
                key, val = keys[i, :, lanes], vals[i, :, lanes]
                query = two_heads(queries[rows, here])
                grad = two_heads(gatt[rows, lanes])
                scores = lax.dot_general(query, key, NT, preferred_element_type=F32) * scale
                expo = jnp.exp(scores - jnp.max(scores, axis=-1, keepdims=True))
                probs = expo / jnp.sum(expo, axis=-1, keepdims=True)
                dprob = lax.dot_general(grad, val, NT, preferred_element_type=F32)
                inner = jnp.sum(probs * dprob, axis=-1, keepdims=True)
                dscore = (probs * (dprob - inner) * scale).astype(BF16)
                attended[rows, lanes] = one_row(
                    jnp.dot(probs.astype(BF16), val, preferred_element_type=F32)
                )
                dquery[rows, lanes] = one_row(jnp.dot(dscore, key, preferred_element_type=F32))
    ordered = jnp.dot(attended[...], order[...], preferred_element_type=F32).astype(BF16)
    for start, stop in SPANS:
        lanes = slice(128 * start, 128 * stop)
        result = flat[:, lanes].astype(F32) + jnp.dot(
            ordered, weights.columns(12, start, stop), preferred_element_type=F32
        )
        block_out[:, :, :, lanes] = result.astype(BF16).reshape(
            images, band_rows, columns, 128 * (stop - start)
        )


def reduce_gradient(
    me, factor, ops, perm, out,
    rcv, gf, gb, r1, h, r2, total, zs, zr, fin,
    op_sems, s1_send, s1_recv, s2_send, s2_recv, z_send, z_recv, o_send, o_recv,
):
    nz, x, y, z, c = me.nz, me.x, me.y, me.z, me.c
    zh = nz // 2
    small = zh * 5
    big = 4 * small
    twin = me.at(c=1 - c)
    mates = [(me.dp, wrap(me.s + k, BANDS)) for k in range(1, BANDS)]
    spans = [pl.ds(128 * a, 128 * (b - a)) for a, b in SPANS]
    send(ops.at[1 - c], rcv, op_sems.at[0], op_sems.at[1], twin)
    own = ops[c]
    lhs_own = jnp.dot(own[0], perm[...], preferred_element_type=F32).astype(BF16)
    await_bytes(rcv, op_sems.at[1])
    lhs_far = jnp.dot(rcv[0], perm[...], preferred_element_type=F32).astype(BF16)
    lhs = jnp.concatenate([lhs_own, lhs_far], axis=0)
    first = c == 0
    a1 = jnp.where(first, y, x)
    a2 = jnp.where(first, x, y)
    active = lax.div(z, zh) == me.xl
    for p, (start, stop) in enumerate(SPANS):
        lanes = slice(128 * start, 128 * stop)
        rhs = jnp.concatenate([own[1][:, lanes], rcv[1, :, lanes]], axis=0)
        grads = lax.dot_general(
            lhs, rhs, (((0,), (0,)), ((), ())), preferred_element_type=F32
        ) * factor
        gf[:, lanes] = grads
        gb[:, lanes] = grads.astype(BF16)
        for k in (2, 1, 3):
            to = wrap(a1 + k, 4)
            device = me.at(x=jnp.where(first, x, to), y=jnp.where(first, to, y))
            send(
                gb.at[pl.ds(pl.multiple_of(to * big, 32), big), spans[p]],
                r1.at[k - 1, :, spans[p]], s1_send.at[p], s1_recv.at[p], device,
            )

    def part_two(p):
        span = spans[p]
        await_bytes(r1.at[:, :, span], s1_recv.at[p])
        acc = gf[pl.ds(pl.multiple_of(a1 * big, 32), big), span]
        for k in range(3):
            acc = acc + r1[k, :, span].astype(F32)
        h[:, span] = acc
        for k in (2, 1, 3):
            to = wrap(a2 + k, 4)
            device = me.at(x=jnp.where(first, to, x), y=jnp.where(first, y, to))
            send(
                h.at[pl.ds(pl.multiple_of(to * small, 8), small), span],
                r2.at[k - 1, :, span], s2_send.at[p], s2_recv.at[p], device,
            )

    def part_three(p):
        span = spans[p]
        await_bytes(r2.at[:, :, span], s2_recv.at[p])
        acc = h[pl.ds(pl.multiple_of(a2 * small, 8), small), span]
        for k in range(3):
            acc = acc + r2[k, :, span]
        total[:, span] = acc
        for i in range(zh):
            zs[i, 0:5, span] = total[5 * i:5 * i + 5, span]
        for i in range(zh):
            to = me.xl * zh + i

            @pl.when(to != z)
            def _():
                send(
                    zs.at[i, :, span], zr.at[z, :, span],
                    z_send.at[p], z_recv.at[p], me.at(z=to),
                )

    zs[...] = jnp.zeros_like(zs)
    part_two(0)
    part_two(1)
    part_three(0)
    part_two(2)
    part_three(1)
    part_three(2)

    @pl.when(active)
    def _():
        for p, span in enumerate(spans):
            zr[z, :, span] = zs[z - me.xl * zh, :, span]
            await_bytes(zr.at[pl.ds(0, nz - 1), :, span], z_recv.at[p])
            piece = zr[0, :, span]
            for i in range(1, nz):
                piece = piece + zr[i, :, span]
            fin[:, span] = piece
            for mate in mates:
                send(
                    fin.at[:, span], out.at[c * NY + y, :, span], o_send.at[p], o_recv.at[p], mate
                )
            out[c * NY + y, :, span] = piece
        for p, span in enumerate(spans):
            await_bytes(out.at[pl.ds(0, CORE - 1), :, span], o_recv.at[p])
            await_bytes(zr.at[pl.ds(0, BANDS - 1), :, span], o_send.at[p])
            await_bytes(zs.at[pl.ds(0, zh - 1), :, span], z_send.at[p])

    @pl.when(jnp.logical_not(active))
    def _():
        for p, span in enumerate(spans):
            await_bytes(out.at[:, :, span], o_recv.at[p])
            await_bytes(zs.at[:, :, span], z_send.at[p])

    await_bytes(rcv, op_sems.at[0])
    for p, span in enumerate(spans):
        await_bytes(r1.at[:, :, span], s1_send.at[p])
        await_bytes(r2.at[:, :, span], s2_send.at[p])


def block_kernel(
    nz, factor,
    lat, plan, conv, attn, gain, cot,
    block_out, grad_out,
    wmain, wext, wleft, wslice, extra, spare, sums, planb, halo, sbuf, order, perm,
    taps, keys, vals, gatt, ops,
    rcv, gf, gb, r1, h, r2, total, zs, zr, fin,
    z_send, z_recv, x_sems, a_send, b_send, c_send, d_send, f_send,
    a_recv, b_recv, c_recv, d_recv, f_recv, misc_send, misc_recv,
    op_sems, s1_send, s1_recv, s2_send, s2_recv, g_send, g_recv, o_send, o_recv,
):
    me = Spot(nz)
    x, y, z, c, s = me.x, me.y, me.z, me.c, me.s
    channels = lat.shape[-1]
    rounds = nz // 4
    twin = me.at(c=1 - c)
    north, south = me.at(y=y + 1), me.at(y=y - 1)
    east, west = me.at(x=x + 1), me.at(x=x - 1)
    side = jnp.where(me.xl == 0, -1, 1)
    other_x = me.at(x=x + side)
    mates = [(me.dp, wrap(s + k, BANDS)) for k in range(1, BANDS)]
    greeted = mates + [me.at(z=z + k) for k in range(1, nz)] + [other_x, me.at(x=x + 2)]
    barrier = pltpu.get_barrier_semaphore()
    for device in greeted:
        pl.semaphore_signal(barrier, inc=1, device_id=device, device_id_type=MESH)
    my_sid = me.sid(x, y)
    own_slice(me, conv, attn, wslice, extra, spare)
    band_sums(lat, group_table(channels), sums)
    pl.semaphore_wait(barrier, len(greeted))

    steps = reach(nz)
    for slot, step in enumerate(steps):
        if slot:
            back = steps.index(-step) if -step in steps else slot
            send(
                wslice, wmain.at[my_sid, me.xh, back // 4, back % 4 // 2, back % 2],
                z_send, z_recv.at[back // 4], me.at(z=z + step),
            )
    for mate in mates:
        send(sums, sbuf.at[s], misc_send.at[0], misc_recv.at[0], mate)
    send(lat.at[:, 0], halo.at[1], misc_send.at[1], misc_recv.at[1], (me.dp, wrap(s - 1, BANDS)))
    send(lat.at[:, 1], halo.at[0], misc_send.at[2], misc_recv.at[2], (me.dp, wrap(s + 1, BANDS)))

    @pl.when(c == 0)
    def _():
        for slot, step in enumerate(steps):
            if slot:
                back = steps.index(-step) if -step in steps else slot
                send(extra, wext.at[me.xh, back], x_sems.at[0], x_sems.at[1], me.at(z=z + step))

    pair = (me.dp, ((1 - me.xl) * NY + y) * 2 + c)
    send(plan, planb.at[:, my_sid], misc_send.at[3], misc_recv.at[3], pair)
    for k in (1, 3, 2):
        send(plan, planb.at[:, my_sid], misc_send.at[4], misc_recv.at[4], me.at(y=y + k))

    wmain[my_sid, me.xh, 0, 0, 0] = wslice[...]
    wext[me.xh, 0] = extra[...]
    planb[:, my_sid] = plan[...]
    sbuf[s] = sums[...]
    order[...] = arrival_order(me, channels)
    every = slice(None)

    def block(r, xx, yy, colours, dirs):
        return wmain.at[me.sid(xx, yy), lax.div(wrap(xx, NX), 2), r, colours, dirs]

    def move(r, xx, yy, colours, dirs, send_sem, recv_sem, device):
        ref = block(r, xx, yy, colours, dirs)
        send(ref, ref, send_sem, recv_sem, device)

    def hand_over(r, cells):
        for i, j in cells:
            move(r, x + i, y + j, every, every, f_send, f_recv, twin)

    def units(n):
        return wmain.at[pl.ds(0, n), 0, 0]

    def part_a(r):
        await_bytes(zwait(r), z_recv.at[r])
        for device in (east, west, north, south):
            move(r, x, y, every, every, a_send, a_recv.at[r], device)
        hand_over(r, [(0, 0)])

    def zwait(r):
        return wmain.at[pl.ds(0, 3), 0, 0, 0, 0] if r == 0 else wmain.at[pl.ds(0, 4), 0, 0, 0, 0]

    def part_b(r):
        await_bytes(units(4), a_recv.at[r])
        low, high = pl.ds(0, 1), pl.ds(1, 1)
        move(r, x - 1, y, every, low, b_send, b_recv.at[r], east)
        move(r, x + 1, y, every, high, b_send, b_recv.at[r], west)
        move(r, x, y - 1, every, low, b_send, b_recv.at[r], north)
        move(r, x, y + 1, every, high, b_send, b_recv.at[r], south)
        for k in (1, -1):
            for device in (north, south):
                move(r, x + k, y, low, every, c_send, c_recv.at[r], device)
            for device in (east, west):
                move(r, x, y + k, high, every, c_send, c_recv.at[r], device)
        hand_over(r, [(1, 0), (-1, 0), (0, 1), (0, -1)])

    def part_c(r):
        await_bytes(units(2), b_recv.at[r])
        low, high = pl.ds(0, 1), pl.ds(1, 1)
        for device in (north, south):
            move(r, x + 2, y, low, every, c_send, c_recv.at[r], device)
        for device in (east, west):
            move(r, x, y + 2, high, every, c_send, c_recv.at[r], device)
        hand_over(r, [(2, 0), (0, 2)])

    def part_d(r):
        await_bytes(units(6), c_recv.at[r])
        low, high = pl.ds(0, 1), pl.ds(1, 1)
        for k in (1, -1, 2):
            move(r, x + k, y - 1, low, low, d_send, d_recv.at[r], north)
            move(r, x + k, y + 1, low, high, d_send, d_recv.at[r], south)
            move(r, x - 1, y + k, high, low, d_send, d_recv.at[r], east)
            move(r, x + 1, y + k, high, high, d_send, d_recv.at[r], west)
        hand_over(r, [(1, 1), (1, -1), (-1, 1), (-1, -1)])

    def part_e(r):
        await_bytes(units(3), d_recv.at[r])
        hand_over(r, [(1, 2), (-1, 2), (2, 1), (2, -1), (2, 2)])

    def normalise():
        await_bytes(sbuf.at[pl.ds(0, BANDS - 1)], misc_recv.at[0])
        await_bytes(halo.at[0], misc_recv.at[1])
        await_bytes(halo.at[0], misc_recv.at[2])
        norm_taps(me, lat, gain, halo, sbuf, order, taps)

    def plan_two():
        await_bytes(planb.at[:, 0], misc_recv.at[3])
        theirs = planb.at[:, c * CORE + (1 - me.xl) * NY + y]
        for k in (1, 3, 2):
            send(theirs, theirs, misc_send.at[5], misc_recv.at[5], me.at(y=y + k))

    def plan_three():
        await_bytes(planb.at[:, pl.ds(0, 3)], misc_recv.at[4])
        await_bytes(planb.at[:, pl.ds(0, 3)], misc_recv.at[5])
        mine = planb.at[:, pl.ds(c * CORE, CORE)]
        send(mine, mine, misc_send.at[6], misc_recv.at[6], twin)

    def plan_four():
        await_bytes(planb.at[:, pl.ds(0, CORE)], misc_recv.at[6])
        await_bytes(planb.at[:, pl.ds(0, CORE)], misc_send.at[6])
        await_bytes(planb.at[:, 0], misc_send.at[3])
        await_bytes(planb.at[:, pl.ds(0, 3)], misc_send.at[4])
        await_bytes(planb.at[:, pl.ds(0, 3)], misc_send.at[5])
        order_plan(planb, order)
        perm[...] = scatter_order(me, channels)

    part_a(0)
    plan_two()
    normalise()
    part_b(0)
    for r in range(1, rounds):
        part_a(r)
        part_c(r - 1)
        if r == 1:
            plan_three()
        if r > 1:
            part_e(r - 2)
        part_b(r)
        part_d(r - 1)
        if r == 2:
            plan_four()
    if rounds < 3:
        if rounds < 2:
            plan_three()
        plan_four()
    if rounds > 1:
        part_c(rounds - 1)
        part_e(rounds - 2)
    else:
        part_c(0)

    @pl.when(c == 0)
    def _():
        await_bytes(wext.at[0, pl.ds(0, nz - 1)], x_sems.at[1])
        half = wext.at[me.xh]
        send(half, half, x_sems.at[2], x_sems.at[3], other_x)

    part_d(rounds - 1)
    part_e(rounds - 1)

    @pl.when(c == 0)
    def _():
        await_bytes(wext.at[0], x_sems.at[3])
        send(wext, wext, x_sems.at[4], x_sems.at[5], twin)

    await_bytes(wmain.at[pl.ds(0, CORE)], f_recv)

    @pl.when(c == 0)
    def _():
        await_bytes(wext.at[0, pl.ds(0, nz - 1)], x_sems.at[0])
        await_bytes(wext.at[0], x_sems.at[2])
        await_bytes(wext, x_sems.at[4])

    @pl.when(c != 0)
    def _():
        await_bytes(wext, x_sems.at[5])

    weights = Weights(wmain, wext, wleft)
    weights.gather_left()
    plan_side(cot, planb, weights, order, keys, vals, gatt)
    convolve(lat, weights, taps, ops.at[0, 0])
    attend(
        ops.at[0, 0], weights, order, keys, vals, gatt, ops.at[1, 0], ops.at[0, 1], block_out
    )
    ops[1, 1] = cot[...].reshape(ops.shape[2:])
    reduce_gradient(
        me, factor, ops, perm, grad_out,
        rcv, gf, gb, r1, h, r2, total, zs, zr, fin,
        op_sems, s1_send, s1_recv, s2_send, s2_recv, g_send, g_recv, o_send, o_recv,
    )

    await_bytes(sbuf.at[pl.ds(0, BANDS - 1)], misc_send.at[0])
    await_bytes(halo.at[0], misc_send.at[1])
    await_bytes(halo.at[0], misc_send.at[2])
    await_bytes(wmain.at[pl.ds(0, nz - 1), 0, 0, 0, 0], z_send)
    await_bytes(wmain.at[pl.ds(0, 4), 0], a_send)
    await_bytes(wmain.at[pl.ds(0, 2), 0], b_send)
    await_bytes(wmain.at[pl.ds(0, 6), 0], c_send)
    await_bytes(wmain.at[pl.ds(0, 3), 0], d_send)
    await_bytes(wmain.at[pl.ds(0, CORE)], f_send)


def body(latents, plan, conv_weight, gn_gain, attn_weights, cotangent):
    images, band_rows, columns, channels = latents.shape
    nz = lax.axis_size("dp") // 2
    tokens = images * band_rows * columns
    plan_tokens = BANDS * plan.shape[1]
    factor = 1.0 / math.sqrt(tokens * 2 * nz * BANDS)
    zh = nz // 2
    small, big = 5 * zh, 20 * zh
    rounds = nz // 4
    dma = pltpu.SemaphoreType.DMA
    vmem = pltpu.VMEM
    block_out, pieces = pl.pallas_call(
        functools.partial(block_kernel, nz, factor),
        out_shape=[
            jax.ShapeDtypeStruct(latents.shape, BF16),
            jax.ShapeDtypeStruct((CORE, 8, channels), F32),
        ],
        in_specs=[pl.BlockSpec(memory_space=vmem)] * 6,
        out_specs=[pl.BlockSpec(memory_space=vmem)] * 2,
        scratch_shapes=[
            vmem((BANDS, 2, rounds, 2, 2, UNIT, 128), BF16),
            vmem((2, nz, 32, 128), BF16),
            vmem((65, 2 * nz * 4, 128), BF16),
            vmem((UNIT, 128), BF16),
            vmem((32, 128), BF16),
            vmem((16, 128), F32),
            vmem((8, 128), F32),
            vmem((images, BANDS) + plan.shape[1:], BF16),
            vmem((2, images, columns, channels), BF16),
            vmem((BANDS, 8, 128), F32),
            vmem((channels, channels), BF16),
            vmem((channels, channels), BF16),
            vmem((3, images, band_rows + 2, columns, channels), BF16),
            vmem((images, plan_tokens, channels), BF16),
            vmem((images, plan_tokens, channels), BF16),
            vmem((tokens, channels), BF16),
            vmem((2, 2, tokens, channels), BF16),
            vmem((2, tokens, channels), BF16),
            vmem((4 * big, channels), F32),
            vmem((4 * big, channels), BF16),
            vmem((3, big, channels), BF16),
            vmem((big, channels), F32),
            vmem((3, small, channels), F32),
            vmem((small, channels), F32),
            vmem((zh, 8, channels), F32),
            vmem((max(nz, BANDS), 8, channels), F32),
            vmem((8, channels), F32),
            dma, dma((rounds,)), dma((6,)), dma, dma, dma, dma, dma,
            dma((rounds,)), dma((rounds,)), dma((rounds,)), dma((rounds,)), dma, dma((7,)), dma((7,)),
            dma((2,)), dma((3,)), dma((3,)), dma((3,)), dma((3,)), dma((3,)), dma((3,)),
            dma((3,)), dma((3,)),
        ],
        compiler_params=pltpu.CompilerParams(
            collective_id=0, has_side_effects=True, vmem_limit_bytes=VMEM_LIMIT
        ),
        name="block",
    )(latents, plan, conv_weight, attn_weights, gn_gain[None], cotangent)
    pieces = pieces.reshape(2, NY, 8, channels)[:, :, :5]
    return (block_out, pieces.transpose(1, 2, 0, 3).reshape(20, 2, channels))


def solution(mesh):
    return jax.shard_map(
        body,
        mesh=mesh,
        in_specs=(
            P("dp", "spatial", None, None),
            P("dp", "spatial", None),
            P(None, "dp", None),
            P(),
            P(None, "dp", None),
            P("dp", "spatial", None, None),
        ),
        out_specs=(P("dp", "spatial", None, None), P("dp", None, None)),
        check_vma=False,
    )
```

time: 877 us -> 113 us (0.13)
  waiting for transfers between devices: 732 us -> 0 us
  Pallas kernels: 0 us -> 105 us
  blocking collectives: 52.6 us -> 0 us
  local copies, waits for them, and re-layouts: 39.4 us -> 5.33 us
  matrix products: 31.7 us -> 0 us
  between operations: 14.7 us -> 0.65 us
    all_gather x2 -> x0, waiting for transfers between devices: 303 us -> none  [the longest x1 213 us: body(): lax.all_gather(conv_weight, 'dp', axis=1, tiled=True)]
    unnamed x5 -> x0, waiting for transfers between devices: 286 us -> none
    psum x1 -> x0, waiting for transfers between devices: 143 us -> none  [body(): weight_grads = lax.psum(own_rows, 'spatial')]
    pallas_call x0 -> x1, Pallas kernels: none -> 105 us  [body(): pl.pallas_call(functools.partial(block_kernel, nz, factor), out_shape=[ja...]
    psum x1 -> x0, blocking collectives: 33.4 us -> none  [body(): first_sums, second_sums = lax.psum((first_sums, second_sums), 'spatial')]
    dot_general x11 -> x0, matrix products: 29.1 us -> none  [the longest x1 9.33 us: body(): jnp.einsum('bhnm,bmhe->bnhe', dscore, key_heads, preferred_element_type=j...]
    all_gather x1 -> x0, blocking collectives: 19.2 us -> none  [body(): plan_all = lax.all_gather(plan, 'spatial', axis=1, tiled=True)]
    slice x3 -> x0, local copies, waits for them, and re-layouts: 12.4 us -> none  [the longest x1 12.3 us: body(): weight_o = weights[3]]
  transfers between devices with their start and end apart: 6 -> 0, of which waited for: 4 -> 0; matrix products, arithmetic and copies ran while one was open for 4% -> 0% of each run, Pallas kernels for 0% -> 0%
where the time goes in v2:
time: 113 us; the launch traced here: 111 us
  Pallas kernels  105 us (93%)
  local copies, waits for them, and re-layouts  5.33 us (5%)
    pallas_call x1, Pallas kernels, body(): pl.pallas_call(functools.partial(block_kernel, nz, factor), out_shape=[ja...  105 us
    unnamed x4, local copies, waits for them, and re-layouts  2.41 us

profile of v2, /device:TPU:1, one launch (start us, length us, event | category | flops | bytes accessed | tf_op | source)
XLA Modules:
  0.0 111.4 jit_solution(3625446083165484110)
XLA Ops:
  0.6 1.3 %broadcast_in_dim.3.gain = f32[1,640]{1,0:T(1,128)} reshape(f32[640]{0:T(1024)} %param.9) | data formatting | bytes 5120 | tf_op jit(solution)/shard_map/broadcast_in_dim | solution.py:722
  1.9 1.6 %copy.8.attn = bf16[4,20,640]{2,1,0:T(8,128)(2,1)} copy(bf16[4,20,640]{2,0,1:T(4,128)(2,1)} %param.10) | data formatting | bytes 204800 | tf_op args[4]
  3.5 105.5 %block.1 = (bf16[2,2,32,640]{3,2,1,0:T(8,128)(2,1)}, f32[8,8,640]{2,1,0:T(8,128)}) custom-call(bf16[2,2,32,640]{3,2,1,0:T(8,128)(2,1)} %lat.1, bf16[2,16,640]{2,1,0:T(8,128)(2,1)} %plan.1, bf16[9,20,640]{2,1,0:T(8,128)(2,1)} %conv.1, bf16[4,20,640]{2,1,0:T(8,128)(2,1)} %copy.8.attn, f32[1,640]{1,0:T(1,128)} %broadcast_in_dim.3.gain, bf16[2,2,32,640]{3,2,1,0:T(8,128)(2,1)} %cot.1), custom_call_target="tpu_custom_call" | custom-call | tf_op jit(solution)/shard_map/block/pallas_call | solution.py:677
  108.9 0.9 slice_bitcast_fusion
  109.8 0.0 copy-start
  109.9 0.7 copy.9
  110.6 0.2 copy-done
  110.8 0.7 copy.11
Async XLA Ops:
  109.8 0.9 copy-start

commit v3 on v2

--- a/solution.py
+++ b/solution.py
@@ -116,7 +116,8 @@
     first = me.c == 0
     xx = jnp.where(first, inner, outer)
     yy = jnp.where(first, outer, inner)
-    names = (xx * zh + zi) * SHARD + yy * 5 + i
+    half = floor_of(xx, 2)
+    names = (half * me.nz + 2 * zi + xx - 2 * half) * SHARD + yy * 5 + i
     return one_hot(names, channels)
 
 
@@ -339,16 +340,17 @@
     twin = me.at(c=1 - c)
     mates = [(me.dp, wrap(me.s + k, BANDS)) for k in range(1, BANDS)]
     spans = [pl.ds(128 * a, 128 * (b - a)) for a, b in SPANS]
-    send(ops.at[1 - c], rcv, op_sems.at[0], op_sems.at[1], twin)
+    send(ops.at[1 - c, c], rcv.at[c], op_sems.at[2], op_sems.at[3], twin)
     own = ops[c]
     lhs_own = jnp.dot(own[0], perm[...], preferred_element_type=F32).astype(BF16)
-    await_bytes(rcv, op_sems.at[1])
+    await_bytes(rcv.at[0], op_sems.at[1])
+    await_bytes(rcv.at[0], op_sems.at[3])
     lhs_far = jnp.dot(rcv[0], perm[...], preferred_element_type=F32).astype(BF16)
     lhs = jnp.concatenate([lhs_own, lhs_far], axis=0)
     first = c == 0
     a1 = jnp.where(first, y, x)
     a2 = jnp.where(first, x, y)
-    active = lax.div(z, zh) == me.xl
+    active = lax.rem(z, 2) == me.xl
     for p, (start, stop) in enumerate(SPANS):
         lanes = slice(128 * start, 128 * stop)
         rhs = jnp.concatenate([own[1][:, lanes], rcv[1, :, lanes]], axis=0)
@@ -390,7 +392,7 @@
         for i in range(zh):
             zs[i, 0:5, span] = total[5 * i:5 * i + 5, span]
         for i in range(zh):
-            to = me.xl * zh + i
+            to = 2 * i + me.xl
 
             @pl.when(to != z)
             def _():
@@ -410,7 +412,7 @@
     @pl.when(active)
     def _():
         for p, span in enumerate(spans):
-            zr[z, :, span] = zs[z - me.xl * zh, :, span]
+            zr[z, :, span] = zs[lax.div(z, 2), :, span]
             await_bytes(zr.at[pl.ds(0, nz - 1), :, span], z_recv.at[p])
             piece = zr[0, :, span]
             for i in range(1, nz):
@@ -432,7 +434,8 @@
             await_bytes(out.at[:, :, span], o_recv.at[p])
             await_bytes(zs.at[:, :, span], z_send.at[p])
 
-    await_bytes(rcv, op_sems.at[0])
+    await_bytes(rcv.at[0], op_sems.at[0])
+    await_bytes(rcv.at[0], op_sems.at[2])
     for p, span in enumerate(spans):
         await_bytes(r1.at[:, :, span], s1_send.at[p])
         await_bytes(r2.at[:, :, span], s2_send.at[p])
@@ -444,10 +447,10 @@
     block_out, grad_out,
     wmain, wext, wleft, wslice, extra, spare, sums, planb, halo, sbuf, order, perm,
     taps, keys, vals, gatt, ops,
-    rcv, gf, gb, r1, h, r2, total, zs, zr, fin,
+    rcv, gf, gb, r1, h, r2, total, zs, zr, fin, pieces,
     z_send, z_recv, x_sems, a_send, b_send, c_send, d_send, f_send,
     a_recv, b_recv, c_recv, d_recv, f_recv, misc_send, misc_recv,
-    op_sems, s1_send, s1_recv, s2_send, s2_recv, g_send, g_recv, o_send, o_recv,
+    op_sems, s1_send, s1_recv, s2_send, s2_recv, g_send, g_recv, o_send, o_recv, near,
 ):
     me = Spot(nz)
     x, y, z, c, s = me.x, me.y, me.z, me.c, me.s
@@ -459,7 +462,7 @@
     side = jnp.where(me.xl == 0, -1, 1)
     other_x = me.at(x=x + side)
     mates = [(me.dp, wrap(s + k, BANDS)) for k in range(1, BANDS)]
-    greeted = mates + [me.at(z=z + k) for k in range(1, nz)] + [other_x, me.at(x=x + 2)]
+    greeted = mates + [me.at(z=z + k) for k in (1, -1, 2, -2)] + [other_x, me.at(x=x + 2)]
     barrier = pltpu.get_barrier_semaphore()
     for device in greeted:
         pl.semaphore_signal(barrier, inc=1, device_id=device, device_id_type=MESH)
@@ -469,17 +472,38 @@
     pl.semaphore_wait(barrier, len(greeted))
 
     steps = reach(nz)
-    for slot, step in enumerate(steps):
-        if slot:
-            back = steps.index(-step) if -step in steps else slot
-            send(
-                wslice, wmain.at[my_sid, me.xh, back // 4, back % 4 // 2, back % 2],
-                z_send, z_recv.at[back // 4], me.at(z=z + step),
+
+    def spread(low, high):
+        for slot, step in enumerate(steps):
+            if low < abs(step) <= high:
+                back = steps.index(-step) if -step in steps else slot
+                send(
+                    wslice, wmain.at[my_sid, me.xh, back // 4, back % 4 // 2, back % 2],
+                    z_send, z_recv.at[back // 4], me.at(z=z + step),
+                )
+
+    def widen(k):
+        for step in (k, -k):
+            pl.semaphore_signal(
+                near.at[k // 4], inc=1, device_id=me.at(z=z + step), device_id_type=MESH
             )
+
+    spread(0, 2)
+    widen(2)
     for mate in mates:
         send(sums, sbuf.at[s], misc_send.at[0], misc_recv.at[0], mate)
     send(lat.at[:, 0], halo.at[1], misc_send.at[1], misc_recv.at[1], (me.dp, wrap(s - 1, BANDS)))
     send(lat.at[:, 1], halo.at[0], misc_send.at[2], misc_recv.at[2], (me.dp, wrap(s + 1, BANDS)))
+    pair = (me.dp, ((1 - me.xl) * NY + y) * 2 + c)
+    send(plan, planb.at[:, my_sid], misc_send.at[3], misc_recv.at[3], pair)
+    for k in (1, 3, 2):
+        send(plan, planb.at[:, my_sid], misc_send.at[4], misc_recv.at[4], me.at(y=y + k))
+    pl.semaphore_wait(near.at[0], 2)
+    spread(2, 4)
+    widen(4)
+    order[...] = arrival_order(me, channels)
+    pl.semaphore_wait(near.at[1], 2)
+    spread(4, nz)
 
     @pl.when(c == 0)
     def _():
@@ -488,16 +512,11 @@
                 back = steps.index(-step) if -step in steps else slot
                 send(extra, wext.at[me.xh, back], x_sems.at[0], x_sems.at[1], me.at(z=z + step))
 
-    pair = (me.dp, ((1 - me.xl) * NY + y) * 2 + c)
-    send(plan, planb.at[:, my_sid], misc_send.at[3], misc_recv.at[3], pair)
-    for k in (1, 3, 2):
-        send(plan, planb.at[:, my_sid], misc_send.at[4], misc_recv.at[4], me.at(y=y + k))
-
     wmain[my_sid, me.xh, 0, 0, 0] = wslice[...]
     wext[me.xh, 0] = extra[...]
     planb[:, my_sid] = plan[...]
     sbuf[s] = sums[...]
-    order[...] = arrival_order(me, channels)
+    ops[1, 1] = cot[...].reshape(ops.shape[2:])
     every = slice(None)
 
     def block(r, xx, yy, colours, dirs):
@@ -588,29 +607,26 @@
         perm[...] = scatter_order(me, channels)
 
     part_a(0)
+    part_b(0)
     plan_two()
+    part_a(1)
     normalise()
-    part_b(0)
-    for r in range(1, rounds):
-        part_a(r)
-        part_c(r - 1)
-        if r == 1:
-            plan_three()
-        if r > 1:
-            part_e(r - 2)
-        part_b(r)
-        part_d(r - 1)
-        if r == 2:
-            plan_four()
-    if rounds < 3:
-        if rounds < 2:
-            plan_three()
-        plan_four()
-    if rounds > 1:
-        part_c(rounds - 1)
-        part_e(rounds - 2)
-    else:
-        part_c(0)
+    part_c(0)
+    part_b(1)
+    part_d(0)
+    part_a(2)
+    part_c(1)
+    part_a(3)
+    plan_three()
+    part_e(0)
+    part_b(2)
+    part_d(1)
+    part_b(3)
+    part_c(2)
+    part_e(1)
+    plan_four()
+    part_c(3)
+    part_d(2)
 
     @pl.when(c == 0)
     def _():
@@ -618,8 +634,9 @@
         half = wext.at[me.xh]
         send(half, half, x_sems.at[2], x_sems.at[3], other_x)
 
-    part_d(rounds - 1)
-    part_e(rounds - 1)
+    part_d(3)
+    part_e(2)
+    part_e(3)
 
     @pl.when(c == 0)
     def _():
@@ -642,15 +659,19 @@
     weights.gather_left()
     plan_side(cot, planb, weights, order, keys, vals, gatt)
     convolve(lat, weights, taps, ops.at[0, 0])
+    send(ops.at[1 - c, 1 - c], rcv.at[1 - c], op_sems.at[0], op_sems.at[1], twin)
     attend(
         ops.at[0, 0], weights, order, keys, vals, gatt, ops.at[1, 0], ops.at[0, 1], block_out
     )
-    ops[1, 1] = cot[...].reshape(ops.shape[2:])
     reduce_gradient(
-        me, factor, ops, perm, grad_out,
+        me, factor, ops, perm, pieces,
         rcv, gf, gb, r1, h, r2, total, zs, zr, fin,
         op_sems, s1_send, s1_recv, s2_send, s2_recv, g_send, g_recv, o_send, o_recv,
     )
+
+    for g in range(2):
+        for k in range(NY):
+            grad_out[5 * k:5 * k + 5, g, :] = pieces[g * NY + k, 0:5, :]
 
     await_bytes(sbuf.at[pl.ds(0, BANDS - 1)], misc_send.at[0])
     await_bytes(halo.at[0], misc_send.at[1])
@@ -674,11 +695,11 @@
     rounds = nz // 4
     dma = pltpu.SemaphoreType.DMA
     vmem = pltpu.VMEM
-    block_out, pieces = pl.pallas_call(
+    return tuple(pl.pallas_call(
         functools.partial(block_kernel, nz, factor),
         out_shape=[
             jax.ShapeDtypeStruct(latents.shape, BF16),
-            jax.ShapeDtypeStruct((CORE, 8, channels), F32),
+            jax.ShapeDtypeStruct((SHARD, 2, channels), F32),
         ],
         in_specs=[pl.BlockSpec(memory_space=vmem)] * 6,
         out_specs=[pl.BlockSpec(memory_space=vmem)] * 2,
@@ -710,18 +731,17 @@
             vmem((zh, 8, channels), F32),
             vmem((max(nz, BANDS), 8, channels), F32),
             vmem((8, channels), F32),
+            vmem((CORE, 8, channels), F32),
             dma, dma((rounds,)), dma((6,)), dma, dma, dma, dma, dma,
             dma((rounds,)), dma((rounds,)), dma((rounds,)), dma((rounds,)), dma, dma((7,)), dma((7,)),
-            dma((2,)), dma((3,)), dma((3,)), dma((3,)), dma((3,)), dma((3,)), dma((3,)),
-            dma((3,)), dma((3,)),
+            dma((4,)), dma((3,)), dma((3,)), dma((3,)), dma((3,)), dma((3,)), dma((3,)),
+            dma((3,)), dma((3,)), pltpu.SemaphoreType.REGULAR((2,)),
         ],
         compiler_params=pltpu.CompilerParams(
             collective_id=0, has_side_effects=True, vmem_limit_bytes=VMEM_LIMIT
         ),
         name="block",
-    )(latents, plan, conv_weight, attn_weights, gn_gain[None], cotangent)
-    pieces = pieces.reshape(2, NY, 8, channels)[:, :, :5]
-    return (block_out, pieces.transpose(1, 2, 0, 3).reshape(20, 2, channels))
+    )(latents, plan, conv_weight, attn_weights, gn_gain, cotangent))
 
 
 def solution(mesh):

time: 113 us -> 100 us (0.88); the launches traced: 111 us -> 99.9 us
  Pallas kernels: 105 us -> 95.4 us
  local copies, waits for them, and re-layouts: 5.33 us -> 3.83 us
    pallas_call x1, Pallas kernels: 105 us -> 95.4 us  [body(): pl.pallas_call(functools.partial(block_kernel, nz, factor), out_shape=[ja...]
    transpose x2 -> x0, local copies, waits for them, and re-layouts: 1.65 us -> none  [body(): return (block_out, pieces.transpose(1, 2, 0, 3).reshape(20, 2, channels))]
    unnamed x4 -> x5, local copies, waits for them, and re-layouts: 2.41 us -> 3.83 us
    broadcast_in_dim x1 -> x0, local copies, waits for them, and re-layouts: 1.27 us -> none  [body(): gn_gain[None]]
where the time goes in v3:
time: 100 us; the launch traced here: 99.9 us
  Pallas kernels  95.4 us (95%)
  local copies, waits for them, and re-layouts  3.83 us (4%)
    pallas_call x1, Pallas kernels, body(): pl.pallas_call(functools.partial(block_kernel, nz, factor), out_shape=[ja...  95.4 us
    unnamed x5, local copies, waits for them, and re-layouts  3.83 us

profile of v3, /device:TPU:1, one launch (start us, length us, event | category | flops | bytes accessed | tf_op | source)
XLA Modules:
  0.0 99.9 jit_solution(10198934353282210035)
XLA Ops:
  0.6 1.6 %copy.8.attn = bf16[4,20,640]{2,1,0:T(8,128)(2,1)} copy(bf16[4,20,640]{2,0,1:T(4,128)(2,1)} %param.10) | data formatting | bytes 204800 | tf_op args[4]
  2.2 95.4 %block.1 = (bf16[2,2,32,640]{3,2,1,0:T(8,128)(2,1)}, f32[20,2,640]{2,1,0:T(2,128)}) custom-call(bf16[2,2,32,640]{3,2,1,0:T(8,128)(2,1)} %lat.1, bf16[2,16,640]{2,1,0:T(8,128)(2,1)} %plan.1, bf16[9,20,640]{2,1,0:T(8,128)(2,1)} %conv.1, bf16[4,20,640]{2,1,0:T(8,128)(2,1)} %copy.8.attn, f32[640]{0:T(1024)} %gain.1, bf16[2,2,32,640]{3,2,1,0:T(8,128)(2,1)} %cot.1), custom_call_target="tpu_custom_call" | custom-call | tf_op jit(solution)/shard_map/block/pallas_call | solution.py:698
  97.6 0.0 copy-start
  97.6 1.6 %copy.11 = bf16[2,2,32,640]{3,2,1,0:T(8,128)(2,1)} copy(bf16[2,2,32,640]{3,2,1,0:T(8,128)(2,1)} %get-tuple-element.4) | data formatting | bytes 327680
  99.3 0.0 copy-done
  99.3 0.6 copy.12
Async XLA Ops:
  97.6 1.6 %copy-start = (f32[20,2,640]{2,1,0:T(2,128)S(1)}, f32[20,2,640]{2,1,0:T(2,128)}, u32[]{:S(2)}) copy-start(f32[20,2,640]{2,1,0:T(2,128)} %get-tuple-element.5) | copy-start | bytes 307204

commit v4 on v3

--- a/solution.py
+++ b/solution.py
@@ -19,6 +19,12 @@
 MESH = pl.DeviceIdType.MESH
 VMEM_LIMIT = 62 * 1024 * 1024
 SPANS = ((0, 2), (2, 4), (4, 5))
+GRAD_SPANS = ((0, 3), (3, 5))
+ORDER = (
+    ("a", 0), ("a", 1), ("b", 0), ("plan", 2), ("norm", 0), ("c", 0), ("b", 1), ("d", 0), ("a", 2),
+    ("c", 1), ("a", 3), ("plan", 3), ("e", 0), ("b", 2), ("d", 1), ("b", 3), ("c", 2), ("e", 1),
+    ("left", 0), ("plan", 4), ("c", 3), ("d", 2), ("ext", 0), ("left", 1), ("d", 3), ("e", 2), ("e", 3),
+)
 BF16 = jnp.bfloat16
 F32 = jnp.float32
 NT = (((1,), (1,)), ((), ()))
@@ -48,6 +54,10 @@
         z = self.z if z is None else wrap(z, self.nz)
         c = self.c if c is None else c
         return (lax.div(x, 2) * self.nz + z, (lax.rem(x, 2) * NY + y) * 2 + c)
+
+    def place(self, x, y):
+        at = lax.rem(wrap(x, NX), 2) * NY + wrap(y, NY)
+        return at + jnp.where(at >= 6, 2 * self.c, 0)
 
     def sid(self, x, y):
         return self.c * CORE + lax.rem(wrap(x, NX), 2) * NY + wrap(y, NY)
@@ -129,12 +139,15 @@
 
 def own_slice(me, conv, attn, wslice, extra, spare):
     taps, _, channels = conv.shape
-    per = channels // 128
-    first = 4 * me.sid(me.x, me.y)
+    first = 4 * (me.xl * NY + me.y)
     for j in range(4):
         block = first + j
-        matrix = lax.div(block, per)
-        lanes = pl.ds(pl.multiple_of(lax.rem(block, per) * 128, 128), 128)
+        shared = block - 24 + 8 * me.c
+        alone = block < 24
+        matrix = jnp.where(alone, lax.div(block, 2), jnp.minimum(shared, 12))
+        at = jnp.where(shared < 12, 2, shared - 12)
+        at = jnp.where(alone, lax.rem(block, 2) + 3 * me.c, at)
+        lanes = pl.ds(pl.multiple_of(at * 128, 128), 128)
         one = conv[jnp.minimum(matrix, taps - 1), :, lanes].astype(F32)
         two = attn[jnp.maximum(matrix - taps, 0), :, lanes].astype(F32)
         rows = jnp.where(matrix < taps, one, two)
@@ -159,8 +172,8 @@
     )
 
 
-def norm_taps(me, lat, gain, halo, sbuf, order, taps):
-    images, band_rows, columns, channels = lat.shape
+def norm_taps(me, band_rows, latu, gain, halo, sbuf, order, taps):
+    images, rows, columns, channels = latu.shape
     tot = sbuf[0]
     for i in range(1, BANDS):
         tot = tot + sbuf[i]
@@ -173,20 +186,20 @@
         mean = grouped[i:i + 1] / counted
         variance = grouped[images + i:images + i + 1] / counted - mean * mean
         inverse = lax.rsqrt(variance + eps_norm)
-        for r in range(band_rows + 2):
+        for r in range(rows + 2):
             if r == 0:
                 cells = halo[0, i]
-            elif r == band_rows + 1:
+            elif r == rows + 1:
                 cells = halo[1, i]
             else:
-                cells = lat[i, r - 1]
+                cells = latu[i, r - 1]
             normed = (cells.astype(F32) - mean) * inverse * gain[...]
             hidden = (normed / (1.0 + jnp.exp(-normed))).astype(BF16)
             hidden = jnp.dot(hidden, order[...], preferred_element_type=F32)
             if r == 0:
-                hidden = jnp.where(me.s == 0, 0.0, hidden)
-            if r == band_rows + 1:
-                hidden = jnp.where(me.s == BANDS - 1, 0.0, hidden)
+                hidden = jnp.where(me.s < 2, 0.0, hidden)
+            if r == rows + 1:
+                hidden = jnp.where(me.s >= BANDS - 2, 0.0, hidden)
             before = jnp.where(row_at == 0, 0.0, pltpu.roll(hidden, 1, 0))
             after = jnp.where(row_at == columns - 1, 0.0, pltpu.roll(hidden, columns - 1, 0))
             taps[0, i, r] = before.astype(BF16)
@@ -198,29 +211,35 @@
     def __init__(self, wmain, wext, wleft):
         self.wmain, self.wext, self.wleft = wmain, wext, wleft
 
-    def gather_left(self):
-        wmain, wext, wleft = self.wmain, self.wext, self.wleft
-        count = wmain.shape[1] * wmain.shape[2] * 4
+    def gather_left(self, r):
+        wmain, wleft = self.wmain, self.wleft
+        half = wleft.shape[1] // 2
+
+        def step(sid, carry):
+            tile = wmain[sid, :, r, :, :, 64:80, :].reshape(8, 16, 128).astype(F32)
+            for part in range(2):
+                for which, rows in enumerate(self.paired(tile[:, 8 * part:8 * part + 8])):
+                    rows = rows.reshape(2, 16, 128)
+                    wleft[4 * sid + 2 * part + which, 16 * r:16 * r + 16, :] = rows[0]
+                    wleft[4 * sid + 2 * part + which, half + 16 * r:half + 16 * r + 16, :] = rows[1]
+            return carry
+
+        lax.fori_loop(0, wmain.shape[0], step, 0)
+
+    def gather_ext(self):
+        wext = self.wext
+        count = wext.shape[0] * wext.shape[1]
+        tile = wext[:, :, 16:32, :].reshape(count, 16, 128).astype(F32)
+        self.wleft[self.wleft.shape[0] - 1] = self.paired(tile[:, 0:8])[0]
+
+    def paired(self, tile):
+        count = tile.shape[0]
         low = ints((count // 2, 8, 128), 1) < 4
-
-        def paired(tile):
-            tile = tile.reshape(count // 2, 2, 8, 128)
-            even, odd = tile[:, 0], tile[:, 1]
-            first = jnp.where(low, even, pltpu.roll(odd, 4, 1))
-            second = jnp.where(low, pltpu.roll(even, 4, 1), odd)
-            return [v.reshape(count * 4, 128).astype(BF16) for v in (first, second)]
-
-        def step(sid, carry):
-            tile = wmain[sid, :, :, :, :, 64:80, :].reshape(count, 16, 128).astype(F32)
-            for part in range(2):
-                first, second = paired(tile[:, 8 * part:8 * part + 8])
-                wleft[4 * sid + 2 * part] = first
-                wleft[4 * sid + 2 * part + 1] = second
-            return carry
-
-        lax.fori_loop(0, wmain.shape[0], step, 0)
-        tile = wext[:, :, 16:32, :].reshape(count, 16, 128).astype(F32)
-        wleft[4 * wmain.shape[0]] = paired(tile[:, 0:8])[0]
+        tile = tile.reshape(count // 2, 2, 8, 128)
+        even, odd = tile[:, 0], tile[:, 1]
+        first = jnp.where(low, even, pltpu.roll(odd, 4, 1))
+        second = jnp.where(low, pltpu.roll(even, 4, 1), odd)
+        return [v.reshape(count * 4, 128).astype(BF16) for v in (first, second)]
 
     def block(self, index):
         wmain, wext = self.wmain, self.wext
@@ -231,9 +250,22 @@
             head = wext[:, :, 0:16, :]
         return jnp.concatenate([head.reshape(-1, 128), self.wleft[index]], axis=0)
 
-    def columns(self, matrix, start, stop):
-        parts = [self.block(5 * matrix + n) for n in range(start, stop)]
+    def alone(self, matrix):
+        return jnp.concatenate([self.block(2 * matrix), self.block(2 * matrix + 1)], axis=1)
+
+    def shared(self, start, stop):
+        parts = [self.block(24 + n) for n in range(start, stop)]
         return parts[0] if len(parts) == 1 else jnp.concatenate(parts, axis=1)
+
+    def out(self, start, stop):
+        return self.shared(12 + start, 12 + stop)
+
+
+def own_lanes(c):
+    return pl.ds(pl.multiple_of(384 * c, 128), 256)
+
+
+MIDDLE = slice(256, 384)
 
 
 def order_plan(planb, order):
@@ -244,46 +276,63 @@
         planb[i] = rows.reshape(bands, plan_rows, channels)
 
 
-def plan_side(cot, planb, weights, order, keys, vals, gatt):
+def plan_side(c, cot, planb, weights, order, keys, vals, gatt):
     images, bands, plan_rows, channels = planb.shape
-    for start, stop in SPANS:
-        lanes = slice(128 * start, 128 * stop)
-        weight_k = weights.columns(10, start, stop)
-        weight_v = weights.columns(11, start, stop)
+    for target, matrix in ((keys, 10), (vals, 11)):
+        weight = weights.alone(matrix)
         for i in range(images):
             rows = planb[i].reshape(bands * plan_rows, channels)
-            keys[i, :, lanes] = jnp.dot(rows, weight_k, preferred_element_type=F32).astype(BF16)
-            vals[i, :, lanes] = jnp.dot(rows, weight_v, preferred_element_type=F32).astype(BF16)
+            part = jnp.dot(rows, weight, preferred_element_type=F32).astype(BF16)
+            target[i, :, own_lanes(c)] = part
+        rows = planb[c].reshape(bands * plan_rows, channels)
+        part = jnp.dot(rows, weights.shared(matrix, matrix + 1), preferred_element_type=F32)
+        target[c, :, MIDDLE] = part.astype(BF16)
     total = None
-    flat = cot[...].reshape(-1, channels)
+    flat = cot[...]
     for start, stop in SPANS:
         part = lax.dot_general(
-            flat[:, 128 * start:128 * stop], weights.columns(12, start, stop), NT,
+            flat[:, 128 * start:128 * stop], weights.out(start, stop), NT,
             preferred_element_type=F32,
         )
         total = part if total is None else total + part
-    total = lax.dot_general(total.astype(BF16), order[...], NT, preferred_element_type=F32)
-    gatt[...] = total.astype(BF16)
-
-
-def convolve(lat, weights, taps, mixed):
-    images, band_rows, columns, channels = lat.shape
-    tokens = images * band_rows * columns
-    flat = lat[...].reshape(tokens, channels)
-    for start, stop in SPANS:
-        lanes = slice(128 * start, 128 * stop)
-        total = None
-        for t in range(9):
-            window = taps[t % 3, :, t // 3:t // 3 + band_rows].reshape(tokens, channels)
-            part = jnp.dot(window, weights.columns(t, start, stop), preferred_element_type=F32)
-            total = part if total is None else total + part
-        mixed[:, lanes] = (flat[:, lanes].astype(F32) + total).astype(BF16)
-
-
-def attend(mixed, weights, order, keys, vals, gatt, attended, dquery, block_out):
-    images, band_rows, columns, channels = block_out.shape
+    total = total.astype(BF16)
+    for lanes, rows in ((own_lanes(c), own_lanes(c)), (MIDDLE, MIDDLE)):
+        part = lax.dot_general(total, order[rows, :], NT, preferred_element_type=F32)
+        gatt[:, lanes] = part.astype(BF16)
+
+
+def convolve(c, band_rows, latu, weights, taps, mixed):
+    images, rows, columns, channels = latu.shape
+    tokens = images * rows * columns
+    total = None
+    for t in range(9):
+        window = taps[t % 3, :, t // 3:t // 3 + rows].reshape(tokens, channels)
+        part = jnp.dot(window, weights.alone(t), preferred_element_type=F32)
+        total = part if total is None else total + part
+    flat = latu[:, :, :, own_lanes(c)].reshape(tokens, 256)
+    mixed[:, own_lanes(c)] = (flat.astype(F32) + total).astype(BF16)
+    total = None
+    first = band_rows * c
+    for t in range(9):
+        window = taps[t % 3, :, pl.ds(t // 3 + first, band_rows)]
+        window = window.reshape(images * band_rows * columns, channels)
+        part = jnp.dot(window, weights.shared(t, t + 1), preferred_element_type=F32)
+        total = part if total is None else total + part
+    flat = latu[:, pl.ds(first, band_rows), :, MIDDLE].reshape(-1, 128)
+    middle = (flat.astype(F32) + total).astype(BF16)
+    cells = band_rows * columns
+    for i in range(images):
+        mixed[own_cells(c, i, cells), MIDDLE] = middle[cells * i:cells * i + cells]
+
+
+def own_cells(c, i, cells):
+    return pl.ds(pl.multiple_of(2 * cells * i + cells * c, 16), cells)
+
+
+def attend(c, mixed, weights, order, keys, vals, gatt, middle, attended, dquery):
+    images = keys.shape[0]
     scale = 1.0 / math.sqrt(HEAD)
-    cells = band_rows * columns
+    cells = mixed.shape[0] // images
     left = ints((cells, 128), 1) < HEAD
     zero = jnp.zeros((cells, 128), BF16)
 
@@ -293,35 +342,45 @@
     def one_row(value):
         return jnp.where(left, value[:cells], value[cells:]).astype(BF16)
 
-    flat = mixed[...]
-    ordered = jnp.dot(flat, order[...], preferred_element_type=F32).astype(BF16)
-    for start, stop in SPANS:
-        queries = jnp.dot(
-            ordered, weights.columns(9, start, stop), preferred_element_type=F32
-        ).astype(BF16)
-        for n in range(start, stop):
-            lanes = slice(128 * n, 128 * n + 128)
-            here = slice(128 * (n - start), 128 * (n - start) + 128)
-            for i in range(images):
-                rows = slice(cells * i, cells * i + cells)
-                key, val = keys[i, :, lanes], vals[i, :, lanes]
-                query = two_heads(queries[rows, here])
-                grad = two_heads(gatt[rows, lanes])
-                scores = lax.dot_general(query, key, NT, preferred_element_type=F32) * scale
-                expo = jnp.exp(scores - jnp.max(scores, axis=-1, keepdims=True))
-                probs = expo / jnp.sum(expo, axis=-1, keepdims=True)
-                dprob = lax.dot_general(grad, val, NT, preferred_element_type=F32)
-                inner = jnp.sum(probs * dprob, axis=-1, keepdims=True)
-                dscore = (probs * (dprob - inner) * scale).astype(BF16)
-                attended[rows, lanes] = one_row(
-                    jnp.dot(probs.astype(BF16), val, preferred_element_type=F32)
-                )
-                dquery[rows, lanes] = one_row(jnp.dot(dscore, key, preferred_element_type=F32))
-    ordered = jnp.dot(attended[...], order[...], preferred_element_type=F32).astype(BF16)
+    def heads(query, i, rows, lanes):
+        key, val = keys[i, :, lanes], vals[i, :, lanes]
+        query, grad = two_heads(query), two_heads(gatt[rows, lanes])
+        scores = lax.dot_general(query, key, NT, preferred_element_type=F32) * scale
+        expo = jnp.exp(scores - jnp.max(scores, axis=-1, keepdims=True))
+        probs = expo / jnp.sum(expo, axis=-1, keepdims=True)
+        dprob = lax.dot_general(grad, val, NT, preferred_element_type=F32)
+        inner = jnp.sum(probs * dprob, axis=-1, keepdims=True)
+        dscore = (probs * (dprob - inner) * scale).astype(BF16)
+        attended[rows, lanes] = one_row(
+            jnp.dot(probs.astype(BF16), val, preferred_element_type=F32)
+        )
+        dquery[rows, lanes] = one_row(jnp.dot(dscore, key, preferred_element_type=F32))
+
+    ordered = jnp.dot(mixed[...], order[...], preferred_element_type=F32).astype(BF16)
+    queries = jnp.dot(ordered, weights.alone(9), preferred_element_type=F32).astype(BF16)
+    middle[...] = jnp.dot(
+        ordered, weights.shared(9, 10), preferred_element_type=F32
+    ).astype(BF16)
+    for n in range(2):
+        lanes = pl.ds(pl.multiple_of(384 * c + 128 * n, 128), 128)
+        for i in range(images):
+            rows = slice(cells * i, cells * i + cells)
+            heads(queries[rows, 128 * n:128 * n + 128], i, rows, lanes)
+    rows = pl.ds(pl.multiple_of(cells * c, 128), cells)
+    heads(middle[rows, :], c, rows, MIDDLE)
+
+
+def project(c, mixed, weights, order, attended, block_out):
+    images, band_rows, columns, channels = block_out.shape
+    cells = band_rows * columns
+    own = [attended[own_cells(c, i, cells), :] for i in range(images)]
+    flat = [mixed[own_cells(c, i, cells), :] for i in range(images)]
+    own, flat = jnp.concatenate(own, axis=0), jnp.concatenate(flat, axis=0)
+    own = jnp.dot(own, order[...], preferred_element_type=F32).astype(BF16)
     for start, stop in SPANS:
         lanes = slice(128 * start, 128 * stop)
         result = flat[:, lanes].astype(F32) + jnp.dot(
-            ordered, weights.columns(12, start, stop), preferred_element_type=F32
+            own, weights.out(start, stop), preferred_element_type=F32
         )
         block_out[:, :, :, lanes] = result.astype(BF16).reshape(
             images, band_rows, columns, 128 * (stop - start)
@@ -329,31 +388,24 @@
 
 
 def reduce_gradient(
-    me, factor, ops, perm, out,
-    rcv, gf, gb, r1, h, r2, total, zs, zr, fin,
-    op_sems, s1_send, s1_recv, s2_send, s2_recv, z_send, z_recv, o_send, o_recv,
+    me, factor, ops, perm, out, meanwhile,
+    gf, gb, r1, h, r2, total, zs, zr, fin,
+    s1_send, s1_recv, s2_send, s2_recv, z_send, z_recv, o_send, o_recv,
 ):
     nz, x, y, z, c = me.nz, me.x, me.y, me.z, me.c
     zh = nz // 2
     small = zh * 5
     big = 4 * small
-    twin = me.at(c=1 - c)
     mates = [(me.dp, wrap(me.s + k, BANDS)) for k in range(1, BANDS)]
-    spans = [pl.ds(128 * a, 128 * (b - a)) for a, b in SPANS]
-    send(ops.at[1 - c, c], rcv.at[c], op_sems.at[2], op_sems.at[3], twin)
-    own = ops[c]
-    lhs_own = jnp.dot(own[0], perm[...], preferred_element_type=F32).astype(BF16)
-    await_bytes(rcv.at[0], op_sems.at[1])
-    await_bytes(rcv.at[0], op_sems.at[3])
-    lhs_far = jnp.dot(rcv[0], perm[...], preferred_element_type=F32).astype(BF16)
-    lhs = jnp.concatenate([lhs_own, lhs_far], axis=0)
+    spans = [pl.ds(128 * a, 128 * (b - a)) for a, b in GRAD_SPANS]
+    lhs = jnp.dot(ops[c, 0], perm[...], preferred_element_type=F32).astype(BF16)
     first = c == 0
     a1 = jnp.where(first, y, x)
     a2 = jnp.where(first, x, y)
     active = lax.rem(z, 2) == me.xl
-    for p, (start, stop) in enumerate(SPANS):
+    for p, (start, stop) in enumerate(GRAD_SPANS):
         lanes = slice(128 * start, 128 * stop)
-        rhs = jnp.concatenate([own[1][:, lanes], rcv[1, :, lanes]], axis=0)
+        rhs = ops[c, 1, :, lanes]
         grads = lax.dot_general(
             lhs, rhs, (((0,), (0,)), ((), ())), preferred_element_type=F32
         ) * factor
@@ -402,12 +454,11 @@
                 )
 
     zs[...] = jnp.zeros_like(zs)
+    meanwhile()
     part_two(0)
     part_two(1)
     part_three(0)
-    part_two(2)
     part_three(1)
-    part_three(2)
 
     @pl.when(active)
     def _():
@@ -434,8 +485,6 @@
             await_bytes(out.at[:, :, span], o_recv.at[p])
             await_bytes(zs.at[:, :, span], z_send.at[p])
 
-    await_bytes(rcv.at[0], op_sems.at[0])
-    await_bytes(rcv.at[0], op_sems.at[2])
     for p, span in enumerate(spans):
         await_bytes(r1.at[:, :, span], s1_send.at[p])
         await_bytes(r2.at[:, :, span], s2_send.at[p])
@@ -446,8 +495,8 @@
     lat, plan, conv, attn, gain, cot,
     block_out, grad_out,
     wmain, wext, wleft, wslice, extra, spare, sums, planb, halo, sbuf, order, perm,
-    taps, keys, vals, gatt, ops,
-    rcv, gf, gb, r1, h, r2, total, zs, zr, fin, pieces,
+    taps, keys, vals, gatt, ops, latu, middle,
+    gf, gb, r1, h, r2, total, zs, zr, fin, pieces,
     z_send, z_recv, x_sems, a_send, b_send, c_send, d_send, f_send,
     a_recv, b_recv, c_recv, d_recv, f_recv, misc_send, misc_recv,
     op_sems, s1_send, s1_recv, s2_send, s2_recv, g_send, g_recv, o_send, o_recv, near,
@@ -466,9 +515,12 @@
     barrier = pltpu.get_barrier_semaphore()
     for device in greeted:
         pl.semaphore_signal(barrier, inc=1, device_id=device, device_id_type=MESH)
-    my_sid = me.sid(x, y)
+    my_sid, my_place = me.sid(x, y), me.place(x, y)
+    images, band_rows, columns, _ = lat.shape
+    cells = band_rows * columns
     own_slice(me, conv, attn, wslice, extra, spare)
-    band_sums(lat, group_table(channels), sums)
+    for i in range(images):
+        ops[1, 1, own_cells(c, i, cells), :] = cot[i].reshape(cells, channels)
     pl.semaphore_wait(barrier, len(greeted))
 
     steps = reach(nz)
@@ -478,7 +530,7 @@
             if low < abs(step) <= high:
                 back = steps.index(-step) if -step in steps else slot
                 send(
-                    wslice, wmain.at[my_sid, me.xh, back // 4, back % 4 // 2, back % 2],
+                    wslice, wmain.at[my_place, me.xh, back // 4, back % 4 // 2, back % 2],
                     z_send, z_recv.at[back // 4], me.at(z=z + step),
                 )
 
@@ -490,17 +542,26 @@
 
     spread(0, 2)
     widen(2)
-    for mate in mates:
-        send(sums, sbuf.at[s], misc_send.at[0], misc_recv.at[0], mate)
-    send(lat.at[:, 0], halo.at[1], misc_send.at[1], misc_recv.at[1], (me.dp, wrap(s - 1, BANDS)))
-    send(lat.at[:, 1], halo.at[0], misc_send.at[2], misc_recv.at[2], (me.dp, wrap(s + 1, BANDS)))
+    chip = wrap(lax.div(s, 2) + 2 * c - 1, BANDS // 2)
+    for core in range(2):
+        send(
+            lat.at[:, c], halo.at[1 - c], misc_send.at[1], misc_recv.at[2 - c],
+            (me.dp, 2 * chip + core),
+        )
+    send(lat, latu.at[:, pl.ds(band_rows * c, band_rows)], misc_send.at[2], misc_recv.at[7], twin)
+    for i in range(images):
+        ref = ops.at[1, 1, own_cells(c, i, cells)]
+        send(ref, ref, op_sems.at[6], op_sems.at[7], twin)
     pair = (me.dp, ((1 - me.xl) * NY + y) * 2 + c)
     send(plan, planb.at[:, my_sid], misc_send.at[3], misc_recv.at[3], pair)
     for k in (1, 3, 2):
         send(plan, planb.at[:, my_sid], misc_send.at[4], misc_recv.at[4], me.at(y=y + k))
+    band_sums(lat, group_table(channels), sums)
     pl.semaphore_wait(near.at[0], 2)
     spread(2, 4)
     widen(4)
+    for mate in mates:
+        send(sums, sbuf.at[s], misc_send.at[0], misc_recv.at[0], mate)
     order[...] = arrival_order(me, channels)
     pl.semaphore_wait(near.at[1], 2)
     spread(4, nz)
@@ -512,23 +573,19 @@
                 back = steps.index(-step) if -step in steps else slot
                 send(extra, wext.at[me.xh, back], x_sems.at[0], x_sems.at[1], me.at(z=z + step))
 
-    wmain[my_sid, me.xh, 0, 0, 0] = wslice[...]
+    wmain[my_place, me.xh, 0, 0, 0] = wslice[...]
+    latu[:, pl.ds(band_rows * c, band_rows)] = lat[...]
     wext[me.xh, 0] = extra[...]
     planb[:, my_sid] = plan[...]
     sbuf[s] = sums[...]
-    ops[1, 1] = cot[...].reshape(ops.shape[2:])
     every = slice(None)
 
     def block(r, xx, yy, colours, dirs):
-        return wmain.at[me.sid(xx, yy), lax.div(wrap(xx, NX), 2), r, colours, dirs]
+        return wmain.at[me.place(xx, yy), lax.div(wrap(xx, NX), 2), r, colours, dirs]
 
     def move(r, xx, yy, colours, dirs, send_sem, recv_sem, device):
         ref = block(r, xx, yy, colours, dirs)
         send(ref, ref, send_sem, recv_sem, device)
-
-    def hand_over(r, cells):
-        for i, j in cells:
-            move(r, x + i, y + j, every, every, f_send, f_recv, twin)
 
     def units(n):
         return wmain.at[pl.ds(0, n), 0, 0]
@@ -537,7 +594,6 @@
         await_bytes(zwait(r), z_recv.at[r])
         for device in (east, west, north, south):
             move(r, x, y, every, every, a_send, a_recv.at[r], device)
-        hand_over(r, [(0, 0)])
 
     def zwait(r):
         return wmain.at[pl.ds(0, 3), 0, 0, 0, 0] if r == 0 else wmain.at[pl.ds(0, 4), 0, 0, 0, 0]
@@ -554,7 +610,6 @@
                 move(r, x + k, y, low, every, c_send, c_recv.at[r], device)
             for device in (east, west):
                 move(r, x, y + k, high, every, c_send, c_recv.at[r], device)
-        hand_over(r, [(1, 0), (-1, 0), (0, 1), (0, -1)])
 
     def part_c(r):
         await_bytes(units(2), b_recv.at[r])
@@ -563,7 +618,6 @@
             move(r, x + 2, y, low, every, c_send, c_recv.at[r], device)
         for device in (east, west):
             move(r, x, y + 2, high, every, c_send, c_recv.at[r], device)
-        hand_over(r, [(2, 0), (0, 2)])
 
     def part_d(r):
         await_bytes(units(6), c_recv.at[r])
@@ -573,17 +627,18 @@
             move(r, x + k, y + 1, low, high, d_send, d_recv.at[r], south)
             move(r, x - 1, y + k, high, low, d_send, d_recv.at[r], east)
             move(r, x + 1, y + k, high, high, d_send, d_recv.at[r], west)
-        hand_over(r, [(1, 1), (1, -1), (-1, 1), (-1, -1)])
 
     def part_e(r):
         await_bytes(units(3), d_recv.at[r])
-        hand_over(r, [(1, 2), (-1, 2), (2, 1), (2, -1), (2, 2)])
+        both = wmain.at[pl.ds(6 + 2 * c, 2), :, r]
+        send(both, both, f_send, f_recv.at[r], twin)
 
     def normalise():
         await_bytes(sbuf.at[pl.ds(0, BANDS - 1)], misc_recv.at[0])
         await_bytes(halo.at[0], misc_recv.at[1])
         await_bytes(halo.at[0], misc_recv.at[2])
-        norm_taps(me, lat, gain, halo, sbuf, order, taps)
+        await_bytes(lat, misc_recv.at[7])
+        norm_taps(me, band_rows, latu, gain, halo, sbuf, order, taps)
 
     def plan_two():
         await_bytes(planb.at[:, 0], misc_recv.at[3])
@@ -606,44 +661,34 @@
         order_plan(planb, order)
         perm[...] = scatter_order(me, channels)
 
-    part_a(0)
-    part_b(0)
-    plan_two()
-    part_a(1)
-    normalise()
-    part_c(0)
-    part_b(1)
-    part_d(0)
-    part_a(2)
-    part_c(1)
-    part_a(3)
-    plan_three()
-    part_e(0)
-    part_b(2)
-    part_d(1)
-    part_b(3)
-    part_c(2)
-    part_e(1)
-    plan_four()
-    part_c(3)
-    part_d(2)
-
-    @pl.when(c == 0)
-    def _():
-        await_bytes(wext.at[0, pl.ds(0, nz - 1)], x_sems.at[1])
-        half = wext.at[me.xh]
-        send(half, half, x_sems.at[2], x_sems.at[3], other_x)
-
-    part_d(3)
-    part_e(2)
-    part_e(3)
+    weights = Weights(wmain, wext, wleft)
+
+    def left(r):
+        await_bytes(wmain.at[pl.ds(0, 2), :, 0], f_recv.at[r])
+        weights.gather_left(r)
+
+    def ext(_):
+        @pl.when(c == 0)
+        def _():
+            await_bytes(wext.at[0, pl.ds(0, nz - 1)], x_sems.at[1])
+            half = wext.at[me.xh]
+            send(half, half, x_sems.at[2], x_sems.at[3], other_x)
+
+    plans = {2: plan_two, 3: plan_three, 4: plan_four}
+    acts = dict(
+        a=part_a, b=part_b, c=part_c, d=part_d, e=part_e, left=left, ext=ext,
+        plan=lambda k: plans[k](), norm=lambda _: normalise(),
+    )
+    for name, r in ORDER:
+        acts[name](r)
 
     @pl.when(c == 0)
     def _():
         await_bytes(wext.at[0], x_sems.at[3])
         send(wext, wext, x_sems.at[4], x_sems.at[5], twin)
 
-    await_bytes(wmain.at[pl.ds(0, CORE)], f_recv)
+    left(2)
+    left(3)
 
     @pl.when(c == 0)
     def _():
@@ -655,33 +700,50 @@
     def _():
         await_bytes(wext, x_sems.at[5])
 
-    weights = Weights(wmain, wext, wleft)
-    weights.gather_left()
-    plan_side(cot, planb, weights, order, keys, vals, gatt)
-    convolve(lat, weights, taps, ops.at[0, 0])
-    send(ops.at[1 - c, 1 - c], rcv.at[1 - c], op_sems.at[0], op_sems.at[1], twin)
-    attend(
-        ops.at[0, 0], weights, order, keys, vals, gatt, ops.at[1, 0], ops.at[0, 1], block_out
-    )
+    weights.gather_ext()
+    mixed, attended, dquery = ops.at[0, 0], ops.at[1, 0], ops.at[0, 1]
+    part = mixed.at[pl.ds(0, images * cells)]
+
+    def swap_columns(ref, own_rows, sem):
+        wide = ref.at[:, own_lanes(c)]
+        send(wide, wide, op_sems.at[sem], op_sems.at[sem + 1], twin)
+        for rows in own_rows:
+            slim = ref.at[rows, MIDDLE]
+            send(slim, slim, op_sems.at[sem], op_sems.at[sem + 1], twin)
+
+    convolve(c, band_rows, latu, weights, taps, mixed)
+    swap_columns(mixed, [own_cells(c, i, cells) for i in range(images)], 0)
+    await_bytes(part, op_sems.at[7])
+    plan_side(c, ops.at[1, 1], planb, weights, order, keys, vals, gatt)
+    await_bytes(part, op_sems.at[1])
+    attend(c, mixed, weights, order, keys, vals, gatt, middle, attended, dquery)
+    image = [pl.ds(pl.multiple_of(2 * cells * c, 128), 2 * cells)]
+    swap_columns(attended, image, 2)
+    swap_columns(dquery, image, 4)
+    await_bytes(part, op_sems.at[3])
+    await_bytes(part, op_sems.at[5])
     reduce_gradient(
         me, factor, ops, perm, pieces,
-        rcv, gf, gb, r1, h, r2, total, zs, zr, fin,
-        op_sems, s1_send, s1_recv, s2_send, s2_recv, g_send, g_recv, o_send, o_recv,
+        lambda: project(c, mixed, weights, order, attended, block_out),
+        gf, gb, r1, h, r2, total, zs, zr, fin,
+        s1_send, s1_recv, s2_send, s2_recv, g_send, g_recv, o_send, o_recv,
     )
+    for sem in (0, 2, 4, 6):
+        await_bytes(part, op_sems.at[sem])
 
     for g in range(2):
         for k in range(NY):
             grad_out[5 * k:5 * k + 5, g, :] = pieces[g * NY + k, 0:5, :]
 
     await_bytes(sbuf.at[pl.ds(0, BANDS - 1)], misc_send.at[0])
-    await_bytes(halo.at[0], misc_send.at[1])
-    await_bytes(halo.at[0], misc_send.at[2])
-    await_bytes(wmain.at[pl.ds(0, nz - 1), 0, 0, 0, 0], z_send)
+    await_bytes(halo, misc_send.at[1])
+    await_bytes(lat, misc_send.at[2])
+    await_bytes(wmain.at[pl.ds(0, 5), 0, pl.ds(0, 3), 0, 0], z_send)
     await_bytes(wmain.at[pl.ds(0, 4), 0], a_send)
     await_bytes(wmain.at[pl.ds(0, 2), 0], b_send)
     await_bytes(wmain.at[pl.ds(0, 6), 0], c_send)
     await_bytes(wmain.at[pl.ds(0, 3), 0], d_send)
-    await_bytes(wmain.at[pl.ds(0, CORE)], f_send)
+    await_bytes(wmain.at[pl.ds(0, 2)], f_send)
 
 
 def body(latents, plan, conv_weight, gn_gain, attn_weights, cotangent):
@@ -704,9 +766,9 @@
         in_specs=[pl.BlockSpec(memory_space=vmem)] * 6,
         out_specs=[pl.BlockSpec(memory_space=vmem)] * 2,
         scratch_shapes=[
-            vmem((BANDS, 2, rounds, 2, 2, UNIT, 128), BF16),
+            vmem((10, 2, rounds, 2, 2, UNIT, 128), BF16),
             vmem((2, nz, 32, 128), BF16),
-            vmem((65, 2 * nz * 4, 128), BF16),
+            vmem((41, 2 * nz * 4, 128), BF16),
             vmem((UNIT, 128), BF16),
             vmem((32, 128), BF16),
             vmem((16, 128), F32),
@@ -716,12 +778,13 @@
             vmem((BANDS, 8, 128), F32),
             vmem((channels, channels), BF16),
             vmem((channels, channels), BF16),
-            vmem((3, images, band_rows + 2, columns, channels), BF16),
+            vmem((3, images, 2 * band_rows + 2, columns, channels), BF16),
             vmem((images, plan_tokens, channels), BF16),
             vmem((images, plan_tokens, channels), BF16),
-            vmem((tokens, channels), BF16),
-            vmem((2, 2, tokens, channels), BF16),
-            vmem((2, tokens, channels), BF16),
+            vmem((2 * tokens, channels), BF16),
+            vmem((2, 2, 2 * tokens, channels), BF16),
+            vmem((images, 2 * band_rows, columns, channels), BF16),
+            vmem((2 * tokens, 128), BF16),
             vmem((4 * big, channels), F32),
             vmem((4 * big, channels), BF16),
             vmem((3, big, channels), BF16),
@@ -733,9 +796,10 @@
             vmem((8, channels), F32),
             vmem((CORE, 8, channels), F32),
             dma, dma((rounds,)), dma((6,)), dma, dma, dma, dma, dma,
-            dma((rounds,)), dma((rounds,)), dma((rounds,)), dma((rounds,)), dma, dma((7,)), dma((7,)),
-            dma((4,)), dma((3,)), dma((3,)), dma((3,)), dma((3,)), dma((3,)), dma((3,)),
-            dma((3,)), dma((3,)), pltpu.SemaphoreType.REGULAR((2,)),
+            dma((rounds,)), dma((rounds,)), dma((rounds,)), dma((rounds,)), dma((rounds,)),
+            dma((7,)), dma((8,)),
+            dma((8,)), dma((2,)), dma((2,)), dma((2,)), dma((2,)), dma((2,)), dma((2,)),
+            dma((2,)), dma((2,)), pltpu.SemaphoreType.REGULAR((2,)),
         ],
         compiler_params=pltpu.CompilerParams(
             collective_id=0, has_side_effects=True, vmem_limit_bytes=VMEM_LIMIT

time: 100 us -> 98.4 us (0.984)
  Pallas kernels: 95.4 us -> 93.7 us
    pallas_call x1, Pallas kernels: 95.4 us -> 93.7 us  [body(): pl.pallas_call(functools.partial(block_kernel, nz, factor), out_shape=[ja...]
where the time goes in v4:
time: 98.4 us; the launch traced here: 98.2 us
  Pallas kernels  93.7 us (95%)
  local copies, waits for them, and re-layouts  3.83 us (4%)
    pallas_call x1, Pallas kernels, body(): pl.pallas_call(functools.partial(block_kernel, nz, factor), out_shape=[ja...  93.7 us
    unnamed x5, local copies, waits for them, and re-layouts  3.83 us

profile of v4, /device:TPU:1, one launch (start us, length us, event | category | flops | bytes accessed | tf_op | source)
XLA Modules:
  0.0 98.2 jit_solution(7209993397099691039)
XLA Ops:
  0.6 1.6 %copy.8.attn = bf16[4,20,640]{2,1,0:T(8,128)(2,1)} copy(bf16[4,20,640]{2,0,1:T(4,128)(2,1)} %param.10) | data formatting | bytes 204800 | tf_op args[4]
  2.2 93.7 %block.1 = (bf16[2,2,32,640]{3,2,1,0:T(8,128)(2,1)}, f32[20,2,640]{2,1,0:T(2,128)}) custom-call(bf16[2,2,32,640]{3,2,1,0:T(8,128)(2,1)} %lat.1, bf16[2,16,640]{2,1,0:T(8,128)(2,1)} %plan.1, bf16[9,20,640]{2,1,0:T(8,128)(2,1)} %conv.1, bf16[4,20,640]{2,1,0:T(8,128)(2,1)} %copy.8.attn, f32[640]{0:T(1024)} %gain.1, bf16[2,2,32,640]{3,2,1,0:T(8,128)(2,1)} %cot.1), custom_call_target="tpu_custom_call" | custom-call | tf_op jit(solution)/shard_map/block/pallas_call | solution.py:760
  95.9 0.0 copy-start
  96.0 1.6 %copy.11 = bf16[2,2,32,640]{3,2,1,0:T(8,128)(2,1)} copy(bf16[2,2,32,640]{3,2,1,0:T(8,128)(2,1)} %get-tuple-element.4) | data formatting | bytes 327680
  97.6 0.0 copy-done
  97.6 0.6 copy.12
Async XLA Ops:
  95.9 1.6 %copy-start = (f32[20,2,640]{2,1,0:T(2,128)S(1)}, f32[20,2,640]{2,1,0:T(2,128)}, u32[]{:S(2)}) copy-start(f32[20,2,640]{2,1,0:T(2,128)} %get-tuple-element.5) | copy-start | bytes 307204

commit v5 on v4

--- a/solution.py
+++ b/solution.py
@@ -23,7 +23,7 @@
 ORDER = (
     ("a", 0), ("a", 1), ("b", 0), ("plan", 2), ("norm", 0), ("c", 0), ("b", 1), ("d", 0), ("a", 2),
     ("c", 1), ("a", 3), ("plan", 3), ("e", 0), ("b", 2), ("d", 1), ("b", 3), ("c", 2), ("e", 1),
-    ("left", 0), ("plan", 4), ("c", 3), ("d", 2), ("ext", 0), ("left", 1), ("d", 3), ("e", 2), ("e", 3),
+    ("left", 0), ("plan", 4), ("c", 3), ("d", 2), ("ext", 0), ("left", 1), ("d", 3), ("e", 2), ("plan", 5), ("e", 3),
 )
 BF16 = jnp.bfloat16
 F32 = jnp.float32
@@ -137,8 +137,11 @@
     return jnp.where(floor_of(rows, channels // GROUPS) == lanes, 1.0, 0.0)
 
 
-def own_slice(me, conv, attn, wslice, extra, spare):
+def own_slice(me, conv, attn, wide, wslice, extra, spare):
     taps, _, channels = conv.shape
+    rows = attn[...].astype(F32)
+    for m in range(attn.shape[1]):
+        wide[m] = rows[:, m, :]
     first = 4 * (me.xl * NY + me.y)
     for j in range(4):
         block = first + j
@@ -149,12 +152,12 @@
         at = jnp.where(alone, lax.rem(block, 2) + 3 * me.c, at)
         lanes = pl.ds(pl.multiple_of(at * 128, 128), 128)
         one = conv[jnp.minimum(matrix, taps - 1), :, lanes].astype(F32)
-        two = attn[jnp.maximum(matrix - taps, 0), :, lanes].astype(F32)
+        two = wide[jnp.maximum(matrix - taps, 0), :, lanes]
         rows = jnp.where(matrix < taps, one, two)
         wslice[16 * j:16 * j + 16, :] = rows[0:16].astype(BF16)
         spare[4 * j:4 * j + 4, :] = rows[16:20]
     wslice[64:80, :] = spare[...].astype(BF16)
-    extra[0:20, :] = attn[attn.shape[0] - 1, :, channels - 128:channels]
+    extra[0:20, :] = wide[attn.shape[1] - 1, :, channels - 128:channels].astype(BF16)
     extra[20:32, :] = jnp.zeros((12, 128), BF16)
 
 
@@ -211,7 +214,7 @@
     def __init__(self, wmain, wext, wleft):
         self.wmain, self.wext, self.wleft = wmain, wext, wleft
 
-    def gather_left(self, r):
+    def gather_left(self, r, first, last):
         wmain, wleft = self.wmain, self.wleft
         half = wleft.shape[1] // 2
 
@@ -224,7 +227,7 @@
                     wleft[4 * sid + 2 * part + which, half + 16 * r:half + 16 * r + 16, :] = rows[1]
             return carry
 
-        lax.fori_loop(0, wmain.shape[0], step, 0)
+        lax.fori_loop(first, last, step, 0)
 
     def gather_ext(self):
         wext = self.wext
@@ -301,7 +304,7 @@
         gatt[:, lanes] = part.astype(BF16)
 
 
-def convolve(c, band_rows, latu, weights, taps, mixed):
+def convolve_alone(c, latu, weights, taps, mixed):
     images, rows, columns, channels = latu.shape
     tokens = images * rows * columns
     total = None
@@ -311,6 +314,10 @@
         total = part if total is None else total + part
     flat = latu[:, :, :, own_lanes(c)].reshape(tokens, 256)
     mixed[:, own_lanes(c)] = (flat.astype(F32) + total).astype(BF16)
+
+
+def convolve_shared(c, band_rows, latu, weights, taps, mixed):
+    images, _, columns, channels = latu.shape
     total = None
     first = band_rows * c
     for t in range(9):
@@ -494,7 +501,7 @@
     nz, factor,
     lat, plan, conv, attn, gain, cot,
     block_out, grad_out,
-    wmain, wext, wleft, wslice, extra, spare, sums, planb, halo, sbuf, order, perm,
+    wmain, wext, wleft, wide, wslice, extra, spare, sums, planb, halo, sbuf, order, perm,
     taps, keys, vals, gatt, ops, latu, middle,
     gf, gb, r1, h, r2, total, zs, zr, fin, pieces,
     z_send, z_recv, x_sems, a_send, b_send, c_send, d_send, f_send,
@@ -518,7 +525,7 @@
     my_sid, my_place = me.sid(x, y), me.place(x, y)
     images, band_rows, columns, _ = lat.shape
     cells = band_rows * columns
-    own_slice(me, conv, attn, wslice, extra, spare)
+    own_slice(me, conv, attn, wide, wslice, extra, spare)
     for i in range(images):
         ops[1, 1, own_cells(c, i, cells), :] = cot[i].reshape(cells, channels)
     pl.semaphore_wait(barrier, len(greeted))
@@ -665,7 +672,7 @@
 
     def left(r):
         await_bytes(wmain.at[pl.ds(0, 2), :, 0], f_recv.at[r])
-        weights.gather_left(r)
+        weights.gather_left(r, 0, 10)
 
     def ext(_):
         @pl.when(c == 0)
@@ -674,7 +681,13 @@
             half = wext.at[me.xh]
             send(half, half, x_sems.at[2], x_sems.at[3], other_x)
 
-    plans = {2: plan_two, 3: plan_three, 4: plan_four}
+    def ext_two():
+        @pl.when(c == 0)
+        def _():
+            await_bytes(wext.at[0], x_sems.at[3])
+            send(wext, wext, x_sems.at[4], x_sems.at[5], twin)
+
+    plans = {5: ext_two, 2: plan_two, 3: plan_three, 4: plan_four}
     acts = dict(
         a=part_a, b=part_b, c=part_c, d=part_d, e=part_e, left=left, ext=ext,
         plan=lambda k: plans[k](), norm=lambda _: normalise(),
@@ -682,25 +695,8 @@
     for name, r in ORDER:
         acts[name](r)
 
-    @pl.when(c == 0)
-    def _():
-        await_bytes(wext.at[0], x_sems.at[3])
-        send(wext, wext, x_sems.at[4], x_sems.at[5], twin)
-
-    left(2)
-    left(3)
-
-    @pl.when(c == 0)
-    def _():
-        await_bytes(wext.at[0, pl.ds(0, nz - 1)], x_sems.at[0])
-        await_bytes(wext.at[0], x_sems.at[2])
-        await_bytes(wext, x_sems.at[4])
-
-    @pl.when(c != 0)
-    def _():
-        await_bytes(wext, x_sems.at[5])
-
-    weights.gather_ext()
+    for r in (2, 3):
+        weights.gather_left(r, 0, 6)
     mixed, attended, dquery = ops.at[0, 0], ops.at[1, 0], ops.at[0, 1]
     part = mixed.at[pl.ds(0, images * cells)]
 
@@ -711,8 +707,28 @@
             slim = ref.at[rows, MIDDLE]
             send(slim, slim, op_sems.at[sem], op_sems.at[sem + 1], twin)
 
-    convolve(c, band_rows, latu, weights, taps, mixed)
-    swap_columns(mixed, [own_cells(c, i, cells) for i in range(images)], 0)
+    convolve_alone(c, latu, weights, taps, mixed)
+    wide = mixed.at[:, own_lanes(c)]
+    send(wide, wide, op_sems.at[0], op_sems.at[1], twin)
+    for r in (2, 3):
+        await_bytes(wmain.at[pl.ds(0, 2), :, 0], f_recv.at[r])
+        weights.gather_left(r, 6, 10)
+    convolve_shared(c, band_rows, latu, weights, taps, mixed)
+    for i in range(images):
+        slim = mixed.at[own_cells(c, i, cells), MIDDLE]
+        send(slim, slim, op_sems.at[0], op_sems.at[1], twin)
+
+    @pl.when(c == 0)
+    def _():
+        await_bytes(wext.at[0, pl.ds(0, nz - 1)], x_sems.at[0])
+        await_bytes(wext.at[0], x_sems.at[2])
+        await_bytes(wext, x_sems.at[4])
+
+    @pl.when(c != 0)
+    def _():
+        await_bytes(wext, x_sems.at[5])
+
+    weights.gather_ext()
     await_bytes(part, op_sems.at[7])
     plan_side(c, ops.at[1, 1], planb, weights, order, keys, vals, gatt)
     await_bytes(part, op_sems.at[1])
@@ -769,6 +785,7 @@
             vmem((10, 2, rounds, 2, 2, UNIT, 128), BF16),
             vmem((2, nz, 32, 128), BF16),
             vmem((41, 2 * nz * 4, 128), BF16),
+            vmem((4, SHARD, channels), F32),
             vmem((UNIT, 128), BF16),
             vmem((32, 128), BF16),
             vmem((16, 128), F32),
@@ -805,7 +822,7 @@
             collective_id=0, has_side_effects=True, vmem_limit_bytes=VMEM_LIMIT
         ),
         name="block",
-    )(latents, plan, conv_weight, attn_weights, gn_gain, cotangent))
+    )(latents, plan, conv_weight, attn_weights.transpose(1, 0, 2), gn_gain, cotangent))
 
 
 def solution(mesh):

time: 98.4 us -> 95.9 us (0.975)
  local copies, waits for them, and re-layouts: 3.83 us -> 2.28 us
    unnamed x5 -> x4, local copies, waits for them, and re-layouts: 3.83 us -> 2.28 us
where the time goes in v5:
time: 95.9 us; the launch traced here: 95.8 us
  Pallas kernels  92.8 us (97%)
  local copies, waits for them, and re-layouts  2.28 us (2%)
    pallas_call x1, Pallas kernels, body(): pl.pallas_call(functools.partial(block_kernel, nz, factor), out_shape=[ja...  92.8 us
    unnamed x4, local copies, waits for them, and re-layouts  2.28 us

profile of v5, /device:TPU:1, one launch (start us, length us, event | category | flops | bytes accessed | tf_op | source)
XLA Modules:
  0.0 95.8 jit_solution(5293703261570533853)
XLA Ops:
  0.6 92.8 %block.1 = (bf16[2,2,32,640]{3,2,1,0:T(8,128)(2,1)}, f32[20,2,640]{2,1,0:T(2,128)}) custom-call(bf16[2,2,32,640]{3,2,1,0:T(8,128)(2,1)} %lat.1, bf16[2,16,640]{2,1,0:T(8,128)(2,1)} %plan.1, bf16[9,20,640]{2,1,0:T(8,128)(2,1)} %conv.1, bf16[20,4,640]{2,1,0:T(4,128)(2,1)} %bitcast.1, f32[640]{0:T(1024)} %gain.1, bf16[2,2,32,640]{3,2,1,0:T(8,128)(2,1)} %cot.1), custom_call_target="tpu_custom_call" | custom-call | tf_op jit(solution)/shard_map/block/pallas_call | solution.py:776
  93.5 0.0 copy-start
  93.5 1.6 %copy.10 = bf16[2,2,32,640]{3,2,1,0:T(8,128)(2,1)} copy(bf16[2,2,32,640]{3,2,1,0:T(8,128)(2,1)} %get-tuple-element.4) | data formatting | bytes 327680
  95.1 0.0 copy-done
  95.1 0.6 copy.11
Async XLA Ops:
  93.5 1.6 %copy-start = (f32[20,2,640]{2,1,0:T(2,128)S(1)}, f32[20,2,640]{2,1,0:T(2,128)}, u32[]{:S(2)}) copy-start(f32[20,2,640]{2,1,0:T(2,128)} %get-tuple-element.5) | copy-start | bytes 307204

commit v6 on v5

--- a/solution.py
+++ b/solution.py
@@ -549,6 +549,8 @@
 
     spread(0, 2)
     widen(2)
+    for device in (east, west, north, south):
+        send(wslice, wmain.at[my_place, me.xh, 0, 0, 0], a_send, a_recv.at[0], device)
     chip = wrap(lax.div(s, 2) + 2 * c - 1, BANDS // 2)
     for core in range(2):
         send(
@@ -600,7 +602,11 @@
     def part_a(r):
         await_bytes(zwait(r), z_recv.at[r])
         for device in (east, west, north, south):
-            move(r, x, y, every, every, a_send, a_recv.at[r], device)
+            if r:
+                move(r, x, y, every, every, a_send, a_recv.at[r], device)
+            else:
+                move(r, x, y, pl.ds(0, 1), pl.ds(1, 1), a_send, a_recv.at[r], device)
+                move(r, x, y, pl.ds(1, 1), every, a_send, a_recv.at[r], device)
 
     def zwait(r):
         return wmain.at[pl.ds(0, 3), 0, 0, 0, 0] if r == 0 else wmain.at[pl.ds(0, 4), 0, 0, 0, 0]

time: 95.9 us -> 96.6 us (level)
  no operation moved by 1% of the time
where the time goes in v6:
time: 96.6 us; the launch traced here: 96.5 us
  Pallas kernels  93.6 us (97%)
  local copies, waits for them, and re-layouts  2.28 us (2%)
    pallas_call x1, Pallas kernels, body(): pl.pallas_call(functools.partial(block_kernel, nz, factor), out_shape=[ja...  93.6 us
    unnamed x4, local copies, waits for them, and re-layouts  2.28 us

profile of v6, /device:TPU:1, one launch (start us, length us, event | category | flops | bytes accessed | tf_op | source)
XLA Modules:
  0.0 96.5 jit_solution(741659223804786990)
XLA Ops:
  0.6 93.6 %block.1 = (bf16[2,2,32,640]{3,2,1,0:T(8,128)(2,1)}, f32[20,2,640]{2,1,0:T(2,128)}) custom-call(bf16[2,2,32,640]{3,2,1,0:T(8,128)(2,1)} %lat.1, bf16[2,16,640]{2,1,0:T(8,128)(2,1)} %plan.1, bf16[9,20,640]{2,1,0:T(8,128)(2,1)} %conv.1, bf16[20,4,640]{2,1,0:T(4,128)(2,1)} %bitcast.1, f32[640]{0:T(1024)} %gain.1, bf16[2,2,32,640]{3,2,1,0:T(8,128)(2,1)} %cot.1), custom_call_target="tpu_custom_call" | custom-call | tf_op jit(solution)/shard_map/block/pallas_call | solution.py:782
  94.2 0.0 copy-start
  94.2 1.6 %copy.10 = bf16[2,2,32,640]{3,2,1,0:T(8,128)(2,1)} copy(bf16[2,2,32,640]{3,2,1,0:T(8,128)(2,1)} %get-tuple-element.4) | data formatting | bytes 327680
  95.8 0.0 copy-done
  95.8 0.6 copy.11
Async XLA Ops:
  94.2 1.6 %copy-start = (f32[20,2,640]{2,1,0:T(2,128)S(1)}, f32[20,2,640]{2,1,0:T(2,128)}, u32[]{:S(2)}) copy-start(f32[20,2,640]{2,1,0:T(2,128)} %get-tuple-element.5) | copy-start | bytes 307204
